TPU v7x, 512 devices: a whole 4x4x16 slice. The times are simulated.
512 devices in a mesh: region: 16 (over y, z_hi, core), tile: 32 (over z_lo, x).
Axes of the slice: x: 4, y: 4, z: 16 (z_hi: 2, z_lo: 8; z = z_hi * 8 + z_lo), core: 2. Of those that a mesh axis runs over, the one named last changes fastest.
Arguments:
- image: bfloat16 [4, 4096, 8192], P(None, 'region', 'tile'), may hold values from -6 to 6
- amplitude: float32 [16, 32, 4, 12, 128], P('region', 'tile'), may hold values from -6 to 6
- positions: int32 [2, 16, 32, 128], P(None, 'region', 'tile'), may hold values from 0 to 255, as said below
- live: int32 [16, 32], P('region', 'tile'), may hold values from 32 to 128, as said below
- psf_rows: bfloat16 [4, 12, 31], replicated, may hold values from -2.5 to 2.5
- psf_cols: bfloat16 [4, 12, 31], replicated, may hold values from -2.5 to 2.5
Outputs:
- updated: float32 [16, 32, 4, 12, 128], P('region', 'tile')
- residual: float32 [4, 4096, 8192], P(None, 'region', 'tile')
Inputs may be any that keep to these rules, and one draw needn't show every extreme that they name: `positions`: every centre lies inside its tile. A source's core reaches past the top edge exactly when its row is below 15, past the bottom edge exactly when its row is above 240, and likewise for columns with 256. The slots of block q = s // 4, for q below 8, hold sources that reach past exactly the edges of direction q, in the order top-left, top, top-right, left, right, bottom-left, bottom, bottom-right; every slot from 32 on holds a source that reaches past no edge. `live`: some tile uses all 128 slots.
All inputs are finite; a program needn't handle non-finite values.
Results may differ from a plain program's by a relative error of at most 0.0011.
Values may be sent and summed in bfloat16 or wider, within the bound.
No kernel may reach another device: no remote copies, remote signals or barrier semaphores. Data moves between devices by JAX's collectives and lax.ppermute only.
A program may use at most 64 MiB of HBM per device.

v0:
```python
import jax
import jax.numpy as jnp
from jax import lax
from jax.sharding import PartitionSpec as P

block_size = 64
step_rate = 0.05


def padded_2(array, sides, width):
    for axis, dim in sides:
        devices, length = (lax.axis_size(axis), array.shape[dim])
        up = [(i, (i + 1) % devices) for i in range(devices - 1)]
        down = [(j, i) for i, j in up]
        last = lax.slice_in_dim(array, length - width, length, axis=dim)
        initial = lax.slice_in_dim(array, 0, width, axis=dim)
        before = lax.ppermute(last, axis, up)
        after = lax.ppermute(initial, axis, down)
        array = jnp.concatenate([before, array, after], axis=dim)
    return array


def place_table(centres, margin, extent, tap_count):
    half_taps = (tap_count - 1) // 2
    shape_all = (tap_count, centres.shape[0], extent)
    tap_index = lax.broadcasted_iota(jnp.int32, shape_all, 0)
    pixel_index = lax.broadcasted_iota(jnp.int32, shape_all, 2)
    return (pixel_index == centres[None, :, None] - half_taps + margin + tap_index).astype(
        jnp.bfloat16
    )


def render_block(canvas, flux_block, centre_rows, centre_cols, margin, psf_rows, psf_cols):
    tap_count = psf_rows.shape[2]
    components = psf_rows.shape[1]
    sources_here = centre_rows.shape[0]
    row_table = place_table(centre_rows, margin, canvas.shape[1], tap_count)
    col_table = place_table(centre_cols, margin, canvas.shape[2], tap_count)
    images = []
    for band_index in range(canvas.shape[0]):
        placed_rows = jnp.einsum(
            "kt,tsy->sky", psf_rows[band_index], row_table, preferred_element_type=jnp.float32
        )
        weighted = (placed_rows * jnp.transpose(flux_block[band_index])[:, :, None]).astype(
            jnp.bfloat16
        )
        placed_cols = jnp.einsum(
            "kt,tsx->skx", psf_cols[band_index], col_table, preferred_element_type=jnp.float32
        ).astype(jnp.bfloat16)
        images.append(
            lax.dot_general(
                weighted.reshape(sources_here * components, -1),
                placed_cols.reshape(sources_here * components, -1),
                (((0,), (0,)), ((), ())),
                preferred_element_type=jnp.float32,
            )
        )
    return canvas + jnp.stack(images)


def gradient_block(padded, centre_rows, centre_cols, margin, psf_rows, psf_cols):
    tap_count = psf_rows.shape[2]
    components = psf_rows.shape[1]
    sources_here = centre_rows.shape[0]
    row_table = place_table(centre_rows, margin, padded.shape[1], tap_count)
    col_table = place_table(centre_cols, margin, padded.shape[2], tap_count)
    results = []
    for band_index in range(padded.shape[0]):
        placed_rows = jnp.einsum(
            "kt,tsy->sky", psf_rows[band_index], row_table, preferred_element_type=jnp.float32
        )
        placed_cols = jnp.einsum(
            "kt,tsx->skx", psf_cols[band_index], col_table, preferred_element_type=jnp.float32
        ).astype(jnp.bfloat16)
        inner = lax.dot_general(
            placed_cols.reshape(sources_here * components, -1),
            padded[band_index],
            (((1,), (1,)), ((), ())),
            preferred_element_type=jnp.float32,
        )
        summed = jnp.sum(placed_rows.reshape(sources_here * components, -1) * inner, axis=1)
        results.append(jnp.transpose(summed.reshape(sources_here, components)))
    return jnp.stack(results)


def on_device(image, amplitude, positions, live, psf_rows, psf_cols):
    fluxes = amplitude[0, 0]
    centres = positions[:, 0, 0]
    capacity = live[0, 0]
    bands, tile_rows, tile_cols = image.shape
    rim_width = (psf_rows.shape[2] - 1) // 2
    block_total = (capacity + block_size - 1) // block_size
    canvas = jnp.zeros((bands, tile_rows + 2 * rim_width, tile_cols + 2 * rim_width), jnp.float32)

    def one_block(block_index, canvas_now):
        start = block_index * block_size
        alive_mask = (start + jnp.arange(block_size, dtype=jnp.int32) < capacity).astype(
            jnp.float32
        )
        flux_block = lax.dynamic_slice_in_dim(fluxes, start, block_size, 2) * alive_mask
        rows_block = lax.dynamic_slice_in_dim(centres[0], start, block_size, 0)
        cols_block = lax.dynamic_slice_in_dim(centres[1], start, block_size, 0)
        return render_block(
            canvas_now, flux_block, rows_block, cols_block, rim_width, psf_rows, psf_cols
        )

    canvas = lax.fori_loop(0, block_total, one_block, canvas)
    edges = jnp.concatenate(
        [canvas[:, :, :rim_width], canvas[:, :, tile_cols + rim_width :]], axis=2
    )
    beside_all = padded_2(edges, (("tile", 2),), rim_width)
    middle = canvas[:, :, rim_width : rim_width + tile_cols]
    middle = middle.at[:, :, :rim_width].add(beside_all[:, :, :rim_width])
    middle = middle.at[:, :, tile_cols - rim_width :].add(beside_all[:, :, 3 * rim_width :])
    strips = jnp.concatenate([middle[:, :rim_width], middle[:, tile_rows + rim_width :]], axis=1)
    beyond = padded_2(strips, (("region", 1),), rim_width)
    model = middle[:, rim_width : rim_width + tile_rows]
    model = model.at[:, :rim_width].add(beyond[:, :rim_width])
    model = model.at[:, tile_rows - rim_width :].add(beyond[:, 3 * rim_width :])
    residual = image.astype(jnp.float32) - model
    rounded = residual.astype(jnp.bfloat16)
    padded = padded_2(rounded, (("region", 1), ("tile", 2)), rim_width)

    def gradient_step(block_index, gradient):
        start = block_index * block_size
        alive_mask = (start + jnp.arange(block_size, dtype=jnp.int32) < capacity).astype(
            jnp.float32
        )
        rows_block = lax.dynamic_slice_in_dim(centres[0], start, block_size, 0)
        cols_block = lax.dynamic_slice_in_dim(centres[1], start, block_size, 0)
        values = (
            gradient_block(padded, rows_block, cols_block, rim_width, psf_rows, psf_cols)
            * alive_mask
        )
        return lax.dynamic_update_slice_in_dim(gradient, values, start, 2)

    gradient = lax.fori_loop(0, block_total, gradient_step, jnp.zeros(fluxes.shape, jnp.float32))
    updated = fluxes + step_rate * gradient
    return (updated[None, None], residual)


def solution(mesh):
    in_specs = (
        P(None, "region", "tile"),
        P("region", "tile", None, None, None),
        P(None, "region", "tile", None),
        P("region", "tile"),
        P(),
        P(),
    )
    out_specs = (P("region", "tile", None, None, None), P(None, "region", "tile"))
    return jax.shard_map(
        on_device, mesh=mesh, in_specs=in_specs, out_specs=out_specs, check_vma=False
    )
```

profile of v0, /device:TPU:11, one launch (start us, length us, event | category | flops | bytes accessed | tf_op | source)
XLA Modules:
  0.0 183.8 jit_solution(9557069788642951225)
XLA Ops:
  1.3 0.7 copy.50
  2.0 0.7 copy.51
  2.9 17.9 %while.34 = (s32[]{:T(128)}, f32[4,286,286]{2,1,0:T(8,128)S(1)}, s32[]{:T(128)}, s32[2,128]{1,0:T(2,128)S(1)}, bf16[4,12,31]{2,1,0:T(8,128)(2,1)S(1)}, /*index=5...) while((s32[]{:T(128)}, f32[4,286,286]{2,1,0:T(8,128)S(1)}, ...), condition=%wide.region_1.2_spmd, body=%wide.region_0.1_spmd.sunk | while | flops 624526592 | bytes 12533683 | solution.py:107
  4.0 0.7 fusion.198
  5.8 0.7 fusion.200
  7.7 0.7 fusion.196
  9.5 0.7 fusion.194
  12.9 0.7 fusion.198
  14.8 0.7 fusion.200
  16.6 0.7 fusion.196
  18.5 0.7 fusion.194
  21.4 0.8 copy.46
  22.2 1.9 %collective-permute-start = (f32[4,286,15]{1,2,0:T(8,128)S(1)}, f32[4,286,15]{1,2,0:T(8,128)S(1)}, u32[]{:S(2)}, u32[]{:S(2)}) collective-permute-start(f32[4,286,15]{1,2,0:T(8,128)S(1)} %get-tuple-element.533), channel_id=1, source_target_pairs={{0,1},{1,2},{2,3},{3,4},{4,5},{5,6},{6,7},{7,8},{8,9},{9,10},{10,1... | collective-permute-start | bytes 205928 | tf_op jit(solution)/shard_map/ppermute | solution.py:17
  24.2 3.4 %collective-permute-start.1 = (f32[4,286,15]{1,2,0:T(8,128)S(1)}, f32[4,286,15]{1,2,0:T(8,128)}, u32[]{:S(2)}, u32[]{:S(2)}) collective-permute-start(f32[4,286,15]{1,2,0:T(8,128)S(1)} %get-tuple-element.532), channel_id=1, source_target_pairs={{1,0},{2,1},{3,2},{4,3},{5,4},{6,5},{7,6},{8,7},{9,8},{10,9},{11,1... | collective-permute-start | bytes 205928 | tf_op jit(solution)/shard_map/ppermute | solution.py:18
  28.0 1.6 collective-permute-done.1
  29.6 0.9 slice_add_fusion.2
  30.8 0.9 fusion.114
  31.7 18.5 %collective-permute-start.2 = (f32[4,15,256]{1,2,0:T(8,128)S(1)}, f32[4,15,256]{1,2,0:T(8,128)}, u32[]{:S(2)}, u32[]{:S(2)}) collective-permute-start(f32[4,15,256]{1,2,0:T(8,128)S(1)} %get-tuple-element.535), channel_id=1, source_target_pairs={{0,32},{32,64},{64,96},{96,128},{128,160},{160,192},{192,224},{224... | collective-permute-start | bytes 184328 | tf_op jit(solution)/shard_map/ppermute | solution.py:17
  50.3 2.0 %copy.42 = bf16[4,256,256]{1,2,0:T(8,128)(2,1)} copy(bf16[4,256,256]{2,1,0:T(8,128)(2,1)} %param.18) | data formatting | bytes 1048576 | tf_op args[0]
  52.7 1.9 %collective-permute-start.3 = (f32[4,15,256]{1,2,0:T(8,128)}, f32[4,15,256]{1,2,0:T(8,128)}, u32[]{:S(2)}, u32[]{:S(2)}) collective-permute-start(f32[4,15,256]{1,2,0:T(8,128)} %get-tuple-element.534), channel_id=1, source_target_pairs={{32,0},{64,32},{96,64},{128,96},{160,128},{192,160},{224,192},{256... | collective-permute-start | bytes 184328 | tf_op jit(solution)/shard_map/ppermute | solution.py:18
  54.6 35.3 %collective-permute-done.2 = f32[4,15,256]{1,2,0:T(8,128)} collective-permute-done((f32[4,15,256]{1,2,0:T(8,128)S(1)}, f32[4,15,256]{1,2,0:T(8,128)}, u32[]{:S(2)}, u32[]{:S(2)}) %collective-permute-start.2) | collective-permute-done | bytes 61472 | tf_op jit(solution)/shard_map/ppermute | solution.py:17
  89.9 1.2 slice_add_fusion.1
  91.1 2.3 %scatter-add.16 = f32[4,256,256]{1,2,0:T(8,128)S(1)} dynamic-update-slice(f32[4,256,256]{1,2,0:T(8,128)S(1)} %slice.431, f32[4,15,256]{1,2,0:T(8,128)S(1)} %slice_add_fusion.1, s32[]{:T(128)} %constant.239.clone.1, s32[]{:T(128)} %constant.239.clone.1, s32[]{:T(128)} %constant.239.clone.1) | dynamic-update-slice | bytes 122884 | tf_op jit(solution)/shard_map/scatter-add | solution.py:118
  93.4 25.0 %collective-permute-done.3 = f32[4,15,256]{1,2,0:T(8,128)} collective-permute-done((f32[4,15,256]{1,2,0:T(8,128)}, f32[4,15,256]{1,2,0:T(8,128)}, u32[]{:S(2)}, u32[]{:S(2)}) %collective-permute-start.3) | collective-permute-done | bytes 61472 | tf_op jit(solution)/shard_map/ppermute | solution.py:18
  118.4 1.2 slice_add_fusion
  119.7 2.4 %scatter-add.19 = f32[4,256,256]{1,2,0:T(8,128)S(1)} dynamic-update-slice(f32[4,256,256]{1,2,0:T(8,128)S(1)} %scatter-add.16, f32[4,15,256]{1,2,0:T(8,128)S(1)} %slice_add_fusion, s32[]{:T(128)} %constant.239.clone.1, s32[]{:T(128)} %constant.245.clone.1, s32[]{:T(128)} %constant.239.clone.1) | dynamic-update-slice | bytes 122884 | tf_op jit(solution)/shard_map/scatter-add | solution.py:119
  122.4 1.9 %collective-permute-start.4 = (bf16[4,15,256]{1,2,0:T(8,128)(2,1)S(1)}, bf16[4,15,256]{1,2,0:T(8,128)(2,1)S(1)}, u32[]{:S(2)}, u32[]{:S(2)}) collective-permute-start(bf16[4,15,256]{1,2,0:T(8,128)(2,1)S(1)} %get-tuple-element.538), channel_id=1, source_target_pairs={{0,32},{32,64},{64,96},{96,128},{128,160},{160,192},{192,224},{224... | collective-permute-start | bytes 92168 | tf_op jit(solution)/shard_map/ppermute | solution.py:17
  124.3 2.4 %collective-permute-start.5 = (bf16[4,15,256]{1,2,0:T(8,128)(2,1)S(1)}, bf16[4,15,256]{1,2,0:T(8,128)(2,1)S(1)}, u32[]{:S(2)}, u32[]{:S(2)}) collective-permute-start(bf16[4,15,256]{1,2,0:T(8,128)(2,1)S(1)} %get-tuple-element.539), channel_id=1, source_target_pairs={{32,0},{64,32},{96,64},{128,96},{160,128},{192,160},{224,192},{256... | collective-permute-start | bytes 92168 | tf_op jit(solution)/shard_map/ppermute | solution.py:18
  126.7 0.9 collective-permute-done.4
  127.6 13.1 %collective-permute-done.5 = bf16[4,15,256]{1,2,0:T(8,128)(2,1)S(1)} collective-permute-done((bf16[4,15,256]{1,2,0:T(8,128)(2,1)S(1)}, bf16[4,15,256]{1,2,0:T(8,128)(2,1)S(1)}, u32[]{:S(2)}, u32[]{:S(2)}) %collective-permute-start.5) | collective-permute-done | bytes 30752 | tf_op jit(solution)/shard_map/ppermute | solution.py:18
  140.8 1.9 %collective-permute-start.6 = (bf16[4,286,15]{1,2,0:T(8,128)(2,1)S(1)}, bf16[4,286,15]{1,2,0:T(8,128)(2,1)S(1)}, u32[]{:S(2)}, u32[]{:S(2)}) collective-permute-start(bf16[4,286,15]{1,2,0:T(8,128)(2,1)S(1)} %get-tuple-element.536), channel_id=1, source_target_pairs={{0,1},{1,2},{2,3},{3,4},{4,5},{5,6},{6,7},{7,8},{8,9},{9,10},{10,1... | collective-permute-start | bytes 102968 | tf_op jit(solution)/shard_map/ppermute | solution.py:17
  142.8 3.5 %collective-permute-start.7 = (bf16[4,286,15]{1,2,0:T(8,128)(2,1)S(1)}, bf16[4,286,15]{1,2,0:T(8,128)(2,1)S(1)}, u32[]{:S(2)}, u32[]{:S(2)}) collective-permute-start(bf16[4,286,15]{1,2,0:T(8,128)(2,1)S(1)} %get-tuple-element.537), channel_id=1, source_target_pairs={{1,0},{2,1},{3,2},{4,3},{5,4},{6,5},{7,6},{8,7},{9,8},{10,9},{11,1... | collective-permute-start | bytes 102968 | tf_op jit(solution)/shard_map/ppermute | solution.py:18
  146.3 1.3 copy.53
  148.3 1.3 copy.52
  149.7 33.6 %while.35 = (s32[]{:T(128)}, f32[4,12,128]{2,0,1:T(4,128)S(1)}, s32[]{:T(128)}, s32[2,128]{1,0:T(2,128)S(1)}, bf16[4,12,31]{2,1,0:T(8,128)(2,1)S(1)}, /*index=5*...) while((s32[]{:T(128)}, f32[4,12,128]{2,0,1:T(4,128)S(1)}, ...), condition=%wide.region_7.8_spmd, body=%wide.region_2.7_spmd.sunk | while | flops 623224000 | bytes 29150900 | solution.py:137
  150.9 0.7 fusion.222
  151.9 1.4 fusion.223
  154.6 0.7 fusion.225
  155.6 1.4 fusion.226
  158.4 0.7 fusion.228
  159.4 1.4 fusion.229
  163.1 1.4 fusion.220
  166.9 0.7 fusion.222
  167.9 1.4 fusion.223
  171.6 1.4 fusion.226
  175.3 1.4 fusion.229
  179.0 1.4 fusion.220
  181.3 1.9 %dynamic_update_slice.11 = f32[4,12,128]{2,0,1:T(4,128)S(1)} dynamic-update-slice(f32[4,12,128]{2,0,1:T(4,128)S(1)} %get-tuple-element.713, f32[4,12,64]{2,0,1:T(4,128)S(1)} %maximum_multiply_fusion.2, s32[]{:T(128)} %constant.239.clone.1..sunk.1, s32[]{:T(128)} %constant.239.clone.1..sunk.1, s32[]{:T(128)S(6)} %select_n.33) | dynamic-update-slice | bytes 24580 | tf_op jit(solution)/shard_map/while/body/dynamic_update_slice | solution.py:135
  (123 shorter events, 32.9 us)
Async XLA Ops:
  0.6 2.2 %copy-start.3 = (s32[2,1,1,128]{3,2,1,0:T(1,128)S(1)}, s32[2,1,1,128]{3,2,1,0:T(1,128)}, u32[]{:S(2)}) copy-start(s32[2,1,1,128]{3,2,1,0:T(1,128)} %param.20) | copy-start | bytes 3076
  0.6 2.2 %copy-start.1 = (f32[1,1,4,12,128]{4,2,3,1,0:T(4,128)S(1)}, f32[1,1,4,12,128]{4,2,3,1,0:T(4,128)}, u32[]{:S(2)}) copy-start(f32[1,1,4,12,128]{4,2,3,1,0:T(4,128)} %param.19) | copy-start | bytes 73732
  20.8 0.6 copy-start.5
  22.2 5.4 %collective-permute-start = (f32[4,286,15]{1,2,0:T(8,128)S(1)}, f32[4,286,15]{1,2,0:T(8,128)S(1)}, u32[]{:S(2)}, u32[]{:S(2)}) collective-permute-start(f32[4,286,15]{1,2,0:T(8,128)S(1)} %get-tuple-element.533), channel_id=1, source_target_pairs={{0,1},{1,2},{2,3},{3,4},{4,5},{5,6},{6,7},{7,8},{8,9},{9,10},{10,1... | collective-permute-start | bytes 205928 | tf_op jit(solution)/shard_map/ppermute | solution.py:17
  24.2 5.5 %collective-permute-start.1 = (f32[4,286,15]{1,2,0:T(8,128)S(1)}, f32[4,286,15]{1,2,0:T(8,128)}, u32[]{:S(2)}, u32[]{:S(2)}) collective-permute-start(f32[4,286,15]{1,2,0:T(8,128)S(1)} %get-tuple-element.532), channel_id=1, source_target_pairs={{1,0},{2,1},{3,2},{4,3},{5,4},{6,5},{7,6},{8,7},{9,8},{10,9},{11,1... | collective-permute-start | bytes 205928 | tf_op jit(solution)/shard_map/ppermute | solution.py:18
  31.7 58.1 %collective-permute-start.2 = (f32[4,15,256]{1,2,0:T(8,128)S(1)}, f32[4,15,256]{1,2,0:T(8,128)}, u32[]{:S(2)}, u32[]{:S(2)}) collective-permute-start(f32[4,15,256]{1,2,0:T(8,128)S(1)} %get-tuple-element.535), channel_id=1, source_target_pairs={{0,32},{32,64},{64,96},{96,128},{128,160},{160,192},{192,224},{224... | collective-permute-start | bytes 184328 | tf_op jit(solution)/shard_map/ppermute | solution.py:17
  52.7 65.8 %collective-permute-start.3 = (f32[4,15,256]{1,2,0:T(8,128)}, f32[4,15,256]{1,2,0:T(8,128)}, u32[]{:S(2)}, u32[]{:S(2)}) collective-permute-start(f32[4,15,256]{1,2,0:T(8,128)} %get-tuple-element.534), channel_id=1, source_target_pairs={{32,0},{64,32},{96,64},{128,96},{160,128},{192,160},{224,192},{256... | collective-permute-start | bytes 184328 | tf_op jit(solution)/shard_map/ppermute | solution.py:18
  93.4 28.7 %copy-start = (bf16[4,256,256]{1,2,0:T(8,128)(2,1)S(1)}, bf16[4,256,256]{1,2,0:T(8,128)(2,1)}, u32[]{:S(2)}) copy-start(bf16[4,256,256]{1,2,0:T(8,128)(2,1)} %copy.42) | copy-start | bytes 1572868
  122.4 5.2 %collective-permute-start.4 = (bf16[4,15,256]{1,2,0:T(8,128)(2,1)S(1)}, bf16[4,15,256]{1,2,0:T(8,128)(2,1)S(1)}, u32[]{:S(2)}, u32[]{:S(2)}) collective-permute-start(bf16[4,15,256]{1,2,0:T(8,128)(2,1)S(1)} %get-tuple-element.538), channel_id=1, source_target_pairs={{0,32},{32,64},{64,96},{96,128},{128,160},{160,192},{192,224},{224... | collective-permute-start | bytes 92168 | tf_op jit(solution)/shard_map/ppermute | solution.py:17
  124.3 16.4 %collective-permute-start.5 = (bf16[4,15,256]{1,2,0:T(8,128)(2,1)S(1)}, bf16[4,15,256]{1,2,0:T(8,128)(2,1)S(1)}, u32[]{:S(2)}, u32[]{:S(2)}) collective-permute-start(bf16[4,15,256]{1,2,0:T(8,128)(2,1)S(1)} %get-tuple-element.539), channel_id=1, source_target_pairs={{32,0},{64,32},{96,64},{128,96},{160,128},{192,160},{224,192},{256... | collective-permute-start | bytes 92168 | tf_op jit(solution)/shard_map/ppermute | solution.py:18
  140.8 6.8 %collective-permute-start.6 = (bf16[4,286,15]{1,2,0:T(8,128)(2,1)S(1)}, bf16[4,286,15]{1,2,0:T(8,128)(2,1)S(1)}, u32[]{:S(2)}, u32[]{:S(2)}) collective-permute-start(bf16[4,286,15]{1,2,0:T(8,128)(2,1)S(1)} %get-tuple-element.536), channel_id=1, source_target_pairs={{0,1},{1,2},{2,3},{3,4},{4,5},{5,6},{6,7},{7,8},{8,9},{9,10},{10,1... | collective-permute-start | bytes 102968 | tf_op jit(solution)/shard_map/ppermute | solution.py:17
  142.8 4.9 %collective-permute-start.7 = (bf16[4,286,15]{1,2,0:T(8,128)(2,1)S(1)}, bf16[4,286,15]{1,2,0:T(8,128)(2,1)S(1)}, u32[]{:S(2)}, u32[]{:S(2)}) collective-permute-start(bf16[4,286,15]{1,2,0:T(8,128)(2,1)S(1)} %get-tuple-element.537), channel_id=1, source_target_pairs={{1,0},{2,1},{3,2},{4,3},{5,4},{6,5},{7,6},{8,7},{9,8},{10,9},{11,1... | collective-permute-start | bytes 102968 | tf_op jit(solution)/shard_map/ppermute | solution.py:18
  147.6 2.0 %copy-start.4 = (s32[2,1,1,128]{3,2,1,0:T(1,128)S(1)}, s32[2,1,1,128]{3,2,1,0:T(1,128)}, u32[]{:S(2)}) copy-start(s32[2,1,1,128]{3,2,1,0:T(1,128)} %param.20) | copy-start | bytes 3076
  147.6 2.0 %copy-start.6 = (bf16[4,12,31]{2,1,0:T(8,128)(2,1)S(1)}, bf16[4,12,31]{2,1,0:T(8,128)(2,1)}, u32[]{:S(2)}) copy-start(bf16[4,12,31]{2,1,0:T(8,128)(2,1)} %copy-done.5) | copy-start | bytes 8932
  149.6 33.6 %copy-start.2 = (f32[1,1,4,12,128]{4,2,3,1,0:T(4,128)S(1)}, f32[1,1,4,12,128]{4,2,3,1,0:T(4,128)}, u32[]{:S(2)}) copy-start(f32[1,1,4,12,128]{4,2,3,1,0:T(4,128)} %param.19) | copy-start | bytes 73732
where the time goes:
time: 185 us; the launch traced here: 184 us
  waiting for transfers between devices  75.9 us (41%)
  matrix products  36.6 us (20%)
  starting transfers between devices  35.5 us (19%)
  local copies, waits for them, and re-layouts  24.8 us (13%)
  other arithmetic  8.66 us (5%)
    ppermute x4, waiting for transfers between devices, padded_2(): after = lax.ppermute(initial, axis, down)  39.8 us
    ppermute x4, waiting for transfers between devices, padded_2(): before = lax.ppermute(last, axis, up)  36.2 us
    ppermute x4, starting transfers between devices, padded_2(): before = lax.ppermute(last, axis, up)  24.3 us
    ppermute x4, starting transfers between devices, padded_2(): after = lax.ppermute(initial, axis, down)  11.2 us
    dot_general x8, matrix products, gradient_block(): lax.dot_general(placed_cols.reshape(sources_here * components, -1), padde...  10.9 us
    dot_general x8, matrix products, render_block(): jnp.einsum('kt,tsy->sky', psf_rows[band_index], row_table, preferred_elem...  5.71 us
    dot_general x8, matrix products, gradient_block(): jnp.einsum('kt,tsx->skx', psf_cols[band_index], col_table, preferred_elem...  5.54 us
    dot_general x8, matrix products, gradient_block(): jnp.einsum('kt,tsy->sky', psf_rows[band_index], row_table, preferred_elem...  5.5 us
  transfers between devices with their start and end apart: 8, of which 5 were waited for; matrix products, arithmetic and copies ran while one was open for 4% of the time, Pallas kernels for 0%

commit v1 on v0

v1 whole, which is shorter than its diff:
```python
import functools

import jax
import jax.numpy as jnp
from jax import lax
from jax.experimental import pallas as pl
from jax.experimental.pallas import tpu as pltpu
from jax.sharding import PartitionSpec as P

step_rate = 0.05
PAD = 16
LANES = 128
CROSS = 32
NT = (((1,), (1,)), ((), ()))
NN = (((1,), (0,)), ((), ()))


def lookup(row, index):
    return jnp.take_along_axis(jnp.broadcast_to(row, index.shape), index, axis=1)


def grouped(value):
    rows = lax.broadcasted_iota(jnp.int32, value.shape, 0)
    total = jnp.where(rows % 4 == 0, value, 0.0)
    for i in range(1, 4):
        total = total + jnp.where(rows % 4 == i, pltpu.roll(value, CROSS * i, axis=1), 0.0)
    return [jnp.sum(total[4 * j : 4 * j + 4], axis=0, keepdims=True) for j in range(3)]


def tap_index(pixel, centre, taps, outside, base=0):
    tap = pixel - centre + (taps - 1) // 2
    return jnp.where((tap >= 0) & (tap < taps), tap, outside) + base


def render_kernel(
    scalars, pos, amp, psf_rows, psf_cols, image,
    field, side, send_a, send_b, table_y, table_x, cross_y, cross_x,
    tmpl_y, tmpl_x, flux, index_y, index_x, scaled, cross_scaled,
):
    bands, comps, taps = psf_rows.shape
    height, width = image.shape[1], image.shape[2]
    ext = height + 2 * PAD
    even = scalars[0] == 0
    live = scalars[2]
    lane = lax.broadcasted_iota(jnp.int32, (1, LANES), 1)
    tmpl_y[...] = jnp.zeros_like(tmpl_y)
    tmpl_x[...] = jnp.zeros_like(tmpl_x)
    tmpl_y[:, :, :taps] = psf_rows[...].astype(jnp.float32)
    tmpl_x[:, :, :taps] = psf_cols[...].astype(jnp.float32)
    flux[...] = jnp.where(lane < live, amp[...], 0.0)
    row, col = pos[0:1, :], pos[1:2, :]
    pixel_y = lax.broadcasted_iota(jnp.int32, (ext, LANES), 0) - PAD
    index_y[...] = tap_index(pixel_y, row, taps, LANES - 1)
    pixel_x = lax.broadcasted_iota(jnp.int32, (width, LANES), 0)
    index_x[...] = tap_index(pixel_x, col, taps, LANES - 1)

    def one_band(b, carry):
        for k in range(comps):
            cut = pl.ds(k * LANES, LANES)
            placed = lookup(tmpl_y[b, k : k + 1, :], index_y[...])
            table_y[b, :, cut] = placed.astype(jnp.bfloat16)
            scaled[:, cut] = (placed * flux[b, k : k + 1, :]).astype(jnp.bfloat16)
            table_x[b, :, cut] = lookup(tmpl_x[b, k : k + 1, :], index_x[...]).astype(jnp.bfloat16)
        model = lax.dot_general(scaled[...], table_x[b], NT, preferred_element_type=jnp.float32)
        field[b] = -model
        field[b, pl.ds(PAD, height), :] += image[b].astype(jnp.float32)
        return carry

    lax.fori_loop(0, bands, one_band, 0)

    first = jnp.where(lane < CROSS, row, 0)
    second = jnp.where(lane < CROSS, col, 0)
    row_four = first
    col_four = second
    for i in range(1, 4):
        row_four = row_four + pltpu.roll(first, CROSS * i, axis=1)
        col_four = col_four + pltpu.roll(second, CROSS * i, axis=1)
    base = (lane // CROSS) * CROSS
    cross_index_y = tap_index(pixel_y, row_four, taps, CROSS - 1, base)
    outer = lax.broadcasted_iota(jnp.int32, (CROSS, LANES), 0)
    outer = jnp.where(outer < PAD, outer - PAD, outer + width - PAD)
    cross_index_x = tap_index(outer, col_four, taps, CROSS - 1, base)
    cross_x[...] = jnp.zeros_like(cross_x)
    for b in range(bands):
        four_y = grouped(tmpl_y[b])
        four_x = grouped(tmpl_x[b])
        four_flux = grouped(jnp.where(lane < CROSS, flux[b], 0.0))
        for j in range(comps // 4):
            cut = pl.ds((b * (comps // 4) + j) * LANES, LANES)
            placed = lookup(four_y[j], cross_index_y)
            cross_y[:, cut] = placed.astype(jnp.bfloat16)
            cross_scaled[:, cut] = (placed * four_flux[j]).astype(jnp.bfloat16)
            cross_x[pl.ds(b * CROSS, CROSS), cut] = lookup(four_x[j], cross_index_x).astype(jnp.bfloat16)
    side[...] = -lax.dot_general(cross_scaled[...], cross_x[...], NT, preferred_element_type=jnp.float32)

    start_a = pl.multiple_of(jnp.where(even, height, 0), 2 * PAD)
    start_b = pl.multiple_of(jnp.where(even, 0, height), 2 * PAD)
    for send, start in ((send_a, start_a), (send_b, start_b)):
        for b in range(bands):
            send[pl.ds(b * 2 * PAD, 2 * PAD), :] = field[b, pl.ds(start, 2 * PAD), :].astype(jnp.bfloat16)
        wide = side[pl.ds(start, 2 * PAD), :].astype(jnp.bfloat16)
        send[pl.ds(bands * 2 * PAD, PAD), pl.ds(0, LANES)] = wide[:PAD]
        send[pl.ds(bands * 2 * PAD, PAD), pl.ds(LANES, LANES)] = wide[PAD:]


def add_rows(scalars, field, side, got_a, got_b):
    bands, ext = field.shape[0], field.shape[1]
    height = ext - 2 * PAD
    even = scalars[0] == 0
    start_a = pl.multiple_of(jnp.where(even, height, 0), 2 * PAD)
    start_b = pl.multiple_of(jnp.where(even, 0, height), 2 * PAD)
    for got, start in ((got_a, start_a), (got_b, start_b)):
        for b in range(bands):
            field[b, pl.ds(start, 2 * PAD), :] += got[pl.ds(b * 2 * PAD, 2 * PAD), :].astype(jnp.float32)
        side[pl.ds(start, PAD), :] += got[pl.ds(bands * 2 * PAD, PAD), pl.ds(0, LANES)].astype(jnp.float32)
        side[pl.ds(start + PAD, PAD), :] += got[pl.ds(bands * 2 * PAD, PAD), pl.ds(LANES, LANES)].astype(jnp.float32)


def column_kernel(scalars, field_in, side_in, got_a, got_b, field, side, send_a, send_b):
    bands, ext, width = field.shape
    field[...] = field_in[...]
    side[...] = side_in[...]
    add_rows(scalars, field, side, got_a, got_b)
    even = scalars[1] == 0
    lane = lax.broadcasted_iota(jnp.int32, (1, LANES), 1)
    to_left = side[...]
    to_right = side[...]
    for b in range(bands):
        low = pltpu.roll(field[b, :, pl.ds(0, LANES)], CROSS * b + PAD, axis=1)
        to_left = jnp.where((lane >= CROSS * b + PAD) & (lane < CROSS * (b + 1)), low, to_left)
        high = pltpu.roll(field[b, :, pl.ds(width - LANES, LANES)], CROSS * b + PAD, axis=1)
        to_right = jnp.where((lane >= CROSS * b) & (lane < CROSS * b + PAD), high, to_right)
    send_a[...] = jnp.where(even, to_right, to_left).astype(jnp.bfloat16)
    send_b[...] = jnp.where(even, to_left, to_right).astype(jnp.bfloat16)


def gradient_kernel(
    scalars, amp, field, side, got_a, got_b, table_y, table_x, cross_y, cross_x,
    updated, residual, total, gradient,
):
    bands, ext, width = field.shape
    height = ext - 2 * PAD
    comps = amp.shape[1]
    even = scalars[1] == 0
    live = scalars[2]
    lane = lax.broadcasted_iota(jnp.int32, (1, LANES), 1)
    from_a, from_b = got_a[...].astype(jnp.float32), got_b[...].astype(jnp.float32)
    from_left = jnp.where(even, from_b, from_a)
    from_right = jnp.where(even, from_a, from_b)
    total[...] = field[...]
    for b in range(bands):
        low = pltpu.roll(from_left, LANES - CROSS * b - PAD, axis=1)
        total[b, :, pl.ds(0, LANES)] += jnp.where(lane < PAD, low, 0.0)
        high = pltpu.roll(from_right, LANES - CROSS * b - PAD, axis=1)
        total[b, :, pl.ds(width - LANES, LANES)] += jnp.where(lane >= LANES - PAD, high, 0.0)
    outer = side[...] + jnp.where(lane % CROSS < PAD, from_left, from_right)
    low_row, high_row, low_col, high_col = scalars[3], scalars[4], scalars[5], scalars[6]
    pixel_y = lax.broadcasted_iota(jnp.int32, (ext, LANES), 0)
    inside = (pixel_y >= low_row) & (pixel_y < high_row)
    inside = inside & (lane % CROSS >= low_col) & (lane % CROSS < high_col)
    outer = jnp.where(inside, outer, 0.0)

    @pl.when(low_row > 0)
    def _():
        total[:, pl.ds(0, PAD), :] = jnp.zeros((bands, PAD, width), jnp.float32)

    @pl.when(high_row < ext)
    def _():
        total[:, pl.ds(ext - PAD, PAD), :] = jnp.zeros((bands, PAD, width), jnp.float32)

    for b in range(bands):
        residual[b] = total[b, pl.ds(PAD, height), :]

    def one_band(b, carry):
        rounded = total[b].astype(jnp.bfloat16)
        for k in range(0, comps, 2):
            cut = pl.ds(k * LANES, 2 * LANES)
            inner = lax.dot_general(rounded, table_x[b, :, cut], NN, preferred_element_type=jnp.float32)
            summed = jnp.sum(inner * table_y[b, :, cut].astype(jnp.float32), axis=0, keepdims=True)
            gradient[b, k : k + 1, :] = summed[:, :LANES]
            gradient[b, k + 1 : k + 2, :] = summed[:, LANES:]
        return carry

    lax.fori_loop(0, bands, one_band, 0)

    inner = lax.dot_general(outer.astype(jnp.bfloat16), cross_x[...], NN, preferred_element_type=jnp.float32)
    summed = jnp.sum(inner * cross_y[...].astype(jnp.float32), axis=0, keepdims=True)
    for b in range(bands):
        for j in range(comps // 4):
            start = (b * (comps // 4) + j) * LANES
            four = summed[:, start : start + LANES]
            for i in range(4):
                part = four if i == 0 else pltpu.roll(four, LANES - CROSS * i, axis=1)
                gradient[b, 4 * j + i : 4 * j + i + 1, :] += jnp.where(lane < CROSS, part, 0.0)
    updated[...] = amp[...] + step_rate * jnp.where(lane < live, gradient[...], 0.0)


SMEM = pl.BlockSpec(memory_space=pltpu.SMEM)
VMEM = pl.BlockSpec(memory_space=pltpu.VMEM)
params = pltpu.CompilerParams(vmem_limit_bytes=48 << 20)


def swaps(axis, first):
    out = []
    for i in range(first, lax.axis_size(axis) - 1, 2):
        out += [(i, i + 1), (i + 1, i)]
    return out


def on_device(image, amplitude, positions, live, psf_rows, psf_cols):
    amp = amplitude[0, 0]
    bands, height, width = image.shape
    comps, slots = amp.shape[1], amp.shape[2]
    ext = height + 2 * PAD
    shape = jax.ShapeDtypeStruct
    f32, bf16 = jnp.float32, jnp.bfloat16
    region, tile = lax.axis_index("region"), lax.axis_index("tile")
    scalars = jnp.stack([
        region % 2,
        tile % 2,
        live[0, 0],
        jnp.where(region == 0, PAD, 0),
        jnp.where(region == lax.axis_size("region") - 1, ext - PAD, ext),
        jnp.where(tile == 0, PAD, 0),
        jnp.where(tile == lax.axis_size("tile") - 1, PAD, 2 * PAD),
    ]).astype(jnp.int32)
    rows_sent = bands * 2 * PAD + PAD
    table_width = comps * slots
    field, side, send_a, send_b, table_y, table_x, cross_y, cross_x = pl.pallas_call(
        render_kernel,
        out_shape=[
            shape((bands, ext, width), f32), shape((ext, LANES), f32),
            shape((rows_sent, width), bf16), shape((rows_sent, width), bf16),
            shape((bands, ext, table_width), bf16), shape((bands, width, table_width), bf16),
            shape((ext, bands * comps * CROSS), bf16), shape((bands * CROSS, bands * comps * CROSS), bf16),
        ],
        in_specs=[SMEM] + [VMEM] * 5,
        out_specs=[VMEM] * 8,
        scratch_shapes=[
            pltpu.VMEM((bands, comps, LANES), f32), pltpu.VMEM((bands, comps, LANES), f32),
            pltpu.VMEM((bands, comps, LANES), f32),
            pltpu.VMEM((ext, LANES), jnp.int32), pltpu.VMEM((width, LANES), jnp.int32),
            pltpu.VMEM((ext, table_width), bf16), pltpu.VMEM((ext, bands * comps * CROSS), bf16),
        ],
        compiler_params=params,
    )(scalars, positions[:, 0, 0], amp, psf_rows, psf_cols, image)
    got_b = lax.ppermute(send_b, "region", swaps("region", 1))
    got_a = lax.ppermute(send_a, "region", swaps("region", 0))
    field, side, send_a, send_b = pl.pallas_call(
        column_kernel,
        out_shape=[
            shape((bands, ext, width), f32), shape((ext, LANES), f32),
            shape((ext, LANES), bf16), shape((ext, LANES), bf16),
        ],
        in_specs=[SMEM] + [VMEM] * 4,
        out_specs=[VMEM] * 4,
        compiler_params=params,
    )(scalars, field, side, got_a, got_b)
    got_b = lax.ppermute(send_b, "tile", swaps("tile", 1))
    got_a = lax.ppermute(send_a, "tile", swaps("tile", 0))
    updated, residual = pl.pallas_call(
        gradient_kernel,
        out_shape=[shape(amp.shape, f32), shape(image.shape, f32)],
        in_specs=[SMEM] + [VMEM] * 9,
        out_specs=[VMEM] * 2,
        scratch_shapes=[
            pltpu.VMEM((bands, ext, width), f32), pltpu.VMEM((bands, comps, LANES), f32),
        ],
        compiler_params=params,
    )(scalars, amp, field, side, got_a, got_b, table_y, table_x, cross_y, cross_x)
    return (updated[None, None], residual)


def solution(mesh):
    in_specs = (
        P(None, "region", "tile"),
        P("region", "tile", None, None, None),
        P(None, "region", "tile", None),
        P("region", "tile"),
        P(),
        P(),
    )
    out_specs = (P("region", "tile", None, None, None), P(None, "region", "tile"))
    return jax.shard_map(
        on_device, mesh=mesh, in_specs=in_specs, out_specs=out_specs, check_vma=False
    )
```

time: 185 us -> 64.1 us (0.35)
  the two profiles are of different devices: /device:TPU:11 before, /device:TPU:56 now
where the time goes in v1:
time: 64.1 us; the launch traced here: 63.6 us
  starting transfers between devices  22.3 us (35%)
  Pallas kernels  20.4 us (32%)
  waiting for transfers between devices  13 us (20%)
  local copies, waits for them, and re-layouts  6.48 us (10%)
  between operations  1.36 us (2%)
    ppermute x1, starting transfers between devices, on_device(): got_b = lax.ppermute(send_b, 'region', swaps('region', 1))  15.1 us
    pallas_call x1, Pallas kernels, on_device(): pl.pallas_call(render_kernel, out_shape=[shape((bands, ext, width), f32),...  15 us
    ppermute x1, waiting for transfers between devices, on_device(): got_b = lax.ppermute(send_b, 'region', swaps('region', 1))  6.58 us
    unnamed x10, local copies, waits for them, and re-layouts  6.39 us
    ppermute x1, waiting for transfers between devices, on_device(): got_b = lax.ppermute(send_b, 'tile', swaps('tile', 1))  5.52 us
    pallas_call x1, Pallas kernels, on_device(): pl.pallas_call(gradient_kernel, out_shape=[shape(amp.shape, f32), shape(i...  4.56 us
    ppermute x1, starting transfers between devices, on_device(): got_a = lax.ppermute(send_a, 'tile', swaps('tile', 0))  3.41 us
    ppermute x1, starting transfers between devices, on_device(): got_b = lax.ppermute(send_b, 'tile', swaps('tile', 1))  1.92 us
  transfers between devices with their start and end apart: 4, of which 3 were waited for; matrix products, arithmetic and copies ran while one was open for 0% of the time, Pallas kernels for 0%

profile of v1, /device:TPU:56, one launch (start us, length us, event | category | flops | bytes accessed | tf_op | source)
XLA Modules:
  0.0 63.6 jit_solution(7790670850279097710)
XLA Ops:
  1.3 0.7 %copy.9.psf_rows = bf16[4,12,31]{2,1,0:T(8,128)(2,1)S(1)} copy(bf16[4,12,31]{2,0,1:T(4,128)(2,1)} %param.10) | data formatting | bytes 5952 | tf_op args[4]
  2.0 0.7 %copy.10.psf_cols = bf16[4,12,31]{2,1,0:T(8,128)(2,1)S(1)} copy(bf16[4,12,31]{2,0,1:T(4,128)(2,1)} %param.11) | data formatting | bytes 5952 | tf_op args[5]
  2.7 0.7 %copy.13 = f32[1,1,4,12,128]{4,3,2,1,0:T(8,128)S(1)} copy(f32[1,1,4,12,128]{4,2,3,1,0:T(4,128)} %param.7) | data formatting | bytes 49152 | tf_op args[1]
  3.5 0.1 stack.27.scalars
  3.5 0.0 copy-start.1
  3.6 1.0 %copy-done.1 = bf16[4,256,256]{2,1,0:T(8,128)(2,1)S(1)} copy-done((bf16[4,256,256]{2,1,0:T(8,128)(2,1)S(1)}, bf16[4,256,256]{2,1,0:T(8,128)(2,1)}, u32[]{:S(2)}) %copy-start.1) | copy-done | bytes 524312
  4.6 0.0 copy-start.2
  4.6 0.7 %copy-done.2 = s32[2,1,1,128]{3,2,1,0:T(1,128)S(1)} copy-done((s32[2,1,1,128]{3,2,1,0:T(1,128)S(1)}, s32[2,1,1,128]{3,2,1,0:T(1,128)}, u32[]{:S(2)}) %copy-start.2) | copy-done | bytes 1048
  5.3 15.0 %shard_map.77 = (f32[4,288,256]{2,1,0:T(8,128)S(1)}, f32[288,128]{1,0:T(8,128)S(1)}, bf16[144,256]{1,0:T(8,128)(2,1)S(1)}, bf16[144,256]{1,0:T(8,128)(2,1)S(1)},...) custom-call(s32[7]{0:T(128)S(1)} %stack.27.scalars, ...), custom_call_target="tpu_custom_call" | custom-call | tf_op jit(solution)/shard_map/pallas_call | solution.py:229
  20.3 1.9 %collective-permute-start = (bf16[144,256]{1,0:T(8,128)(2,1)S(1)}, bf16[144,256]{1,0:T(8,128)(2,1)S(1)}, u32[]{:S(2)}, u32[]{:S(2)}) collective-permute-start(bf16[144,256]{1,0:T(8,128)(2,1)S(1)} %get-tuple-element.18), channel_id=1, source_target_pairs={{0,32},{32,0},{64,96},{96,64},{128,160},{160,128},{192,224},{224,1... | collective-permute-start | bytes 221192 | tf_op jit(solution)/shard_map/ppermute | solution.py:248
  22.2 15.1 %collective-permute-start.1 = (bf16[144,256]{1,0:T(8,128)(2,1)S(1)}, bf16[144,256]{1,0:T(8,128)(2,1)S(1)}, u32[]{:S(2)}, u32[]{:S(2)}) collective-permute-start(bf16[144,256]{1,0:T(8,128)(2,1)S(1)} %get-tuple-element.19), channel_id=1, source_target_pairs={{32,64},{64,32},{96,128},{128,96},{160,192},{192,160},{224,256},{2... | collective-permute-start | bytes 221192 | tf_op jit(solution)/shard_map/ppermute | solution.py:247
  37.3 0.0 collective-permute-done.got_a
  37.3 6.6 %collective-permute-done.1.got_b = bf16[144,256]{1,0:T(8,128)(2,1)S(1)} collective-permute-done((bf16[144,256]{1,0:T(8,128)(2,1)S(1)}, bf16[144,256]{1,0:T(8,128)(2,1)S(1)}, u32[]{:S(2)}, u32[]{:S(2)}) %collective-permute-start.1) | collective-permute-done | bytes 73760 | tf_op jit(solution)/shard_map/ppermute | solution.py:247
  43.9 0.9 %shard_map.78 = (f32[4,288,256]{2,1,0:T(8,128)S(1)}, f32[288,128]{1,0:T(8,128)S(1)}, bf16[288,128]{1,0:T(8,128)(2,1)S(1)}, bf16[288,128]{1,0:T(8,128)(2,1)S(1)}) custom-call(s32[7]{0:T(128)S(1)} %stack.27.scalars, f32[4,288,256]{2,1,0:T(8,128)S(1)} %get-tuple-element.16.field_in, f32[288,128]{1,0:T(8,128)S(1)} %get-tuple-element.17.side_in, ...), custom_call_target="tpu_custom_call" | custom-call | tf_op jit(solution)/shard_map/pallas_call | solution.py:249
  44.8 3.4 %collective-permute-start.2 = (bf16[288,128]{1,0:T(8,128)(2,1)S(1)}, bf16[288,128]{1,0:T(8,128)(2,1)S(1)}, u32[]{:S(2)}, u32[]{:S(2)}) collective-permute-start(bf16[288,128]{1,0:T(8,128)(2,1)S(1)} %get-tuple-element.22), channel_id=1, source_target_pairs={{0,1},{1,0},{2,3},{3,2},{4,5},{5,4},{6,7},{7,6},{8,9},{9,8},{10,11... | collective-permute-start | bytes 221192 | tf_op jit(solution)/shard_map/ppermute | solution.py:260
  48.2 1.9 %collective-permute-start.3 = (bf16[288,128]{1,0:T(8,128)(2,1)S(1)}, bf16[288,128]{1,0:T(8,128)(2,1)S(1)}, u32[]{:S(2)}, u32[]{:S(2)}) collective-permute-start(bf16[288,128]{1,0:T(8,128)(2,1)S(1)} %get-tuple-element.23), channel_id=1, source_target_pairs={{1,2},{2,1},{3,4},{4,3},{5,6},{6,5},{7,8},{8,7},{9,10},{10,9},{11,... | collective-permute-start | bytes 221192 | tf_op jit(solution)/shard_map/ppermute | solution.py:259
  50.1 0.9 %collective-permute-done.2.got_a = bf16[288,128]{1,0:T(8,128)(2,1)S(1)} collective-permute-done((bf16[288,128]{1,0:T(8,128)(2,1)S(1)}, bf16[288,128]{1,0:T(8,128)(2,1)S(1)}, u32[]{:S(2)}, u32[]{:S(2)}) %collective-permute-start.2) | collective-permute-done | bytes 73760 | tf_op jit(solution)/shard_map/ppermute | solution.py:260
  51.0 5.5 %collective-permute-done.3.got_b = bf16[288,128]{1,0:T(8,128)(2,1)S(1)} collective-permute-done((bf16[288,128]{1,0:T(8,128)(2,1)S(1)}, bf16[288,128]{1,0:T(8,128)(2,1)S(1)}, u32[]{:S(2)}, u32[]{:S(2)}) %collective-permute-start.3) | collective-permute-done | bytes 73760 | tf_op jit(solution)/shard_map/ppermute | solution.py:259
  56.6 0.0 copy-start
  56.6 1.9 %copy-done = bf16[4,256,1536]{2,1,0:T(8,128)(2,1)S(1)} copy-done((bf16[4,256,1536]{2,1,0:T(8,128)(2,1)S(1)}, bf16[4,256,1536]{2,1,0:T(8,128)(2,1)}, u32[]{:S(2)}) %copy-start) | copy-done | bytes 3145752
  58.4 4.6 %shard_map.79 = (f32[4,12,128]{2,1,0:T(8,128)S(1)}, f32[4,256,256]{2,1,0:T(8,128)}) custom-call(s32[7]{0:T(128)S(1)} %stack.27.scalars, f32[4,12,128]{2,1,0:T(8,128)S(1)} %bitcast.14, f32[4,288,256]{2,1,0:T(8,128)S(1)} %get-tuple-element.20.field, f32[288,128]{1,0:T(8,128)S(1)} %get-tuple-element.21.side, bf16[288,128]{1,0:T(8,128)(2,1)S(1)} %collective-permute-done.2.got_a, ...), custom_call_target="tpu_custom_call" | custom-call | tf_op jit(solution)/shard_map/pallas_call | solution.py:261
  63.0 0.6 copy.11
Async XLA Ops:
  3.5 1.0 %copy-start.1 = (bf16[4,256,256]{2,1,0:T(8,128)(2,1)S(1)}, bf16[4,256,256]{2,1,0:T(8,128)(2,1)}, u32[]{:S(2)}) copy-start(bf16[4,256,256]{2,1,0:T(8,128)(2,1)} %image.1) | copy-start | bytes 1572868
  4.6 0.7 %copy-start.2 = (s32[2,1,1,128]{3,2,1,0:T(1,128)S(1)}, s32[2,1,1,128]{3,2,1,0:T(1,128)}, u32[]{:S(2)}) copy-start(s32[2,1,1,128]{3,2,1,0:T(1,128)} %param.8) | copy-start | bytes 3076
  20.3 17.0 %collective-permute-start = (bf16[144,256]{1,0:T(8,128)(2,1)S(1)}, bf16[144,256]{1,0:T(8,128)(2,1)S(1)}, u32[]{:S(2)}, u32[]{:S(2)}) collective-permute-start(bf16[144,256]{1,0:T(8,128)(2,1)S(1)} %get-tuple-element.18), channel_id=1, source_target_pairs={{0,32},{32,0},{64,96},{96,64},{128,160},{160,128},{192,224},{224,1... | collective-permute-start | bytes 221192 | tf_op jit(solution)/shard_map/ppermute | solution.py:248
  22.2 21.7 %collective-permute-start.1 = (bf16[144,256]{1,0:T(8,128)(2,1)S(1)}, bf16[144,256]{1,0:T(8,128)(2,1)S(1)}, u32[]{:S(2)}, u32[]{:S(2)}) collective-permute-start(bf16[144,256]{1,0:T(8,128)(2,1)S(1)} %get-tuple-element.19), channel_id=1, source_target_pairs={{32,64},{64,32},{96,128},{128,96},{160,192},{192,160},{224,256},{2... | collective-permute-start | bytes 221192 | tf_op jit(solution)/shard_map/ppermute | solution.py:247
  44.8 6.2 %collective-permute-start.2 = (bf16[288,128]{1,0:T(8,128)(2,1)S(1)}, bf16[288,128]{1,0:T(8,128)(2,1)S(1)}, u32[]{:S(2)}, u32[]{:S(2)}) collective-permute-start(bf16[288,128]{1,0:T(8,128)(2,1)S(1)} %get-tuple-element.22), channel_id=1, source_target_pairs={{0,1},{1,0},{2,3},{3,2},{4,5},{5,4},{6,7},{7,6},{8,9},{9,8},{10,11... | collective-permute-start | bytes 221192 | tf_op jit(solution)/shard_map/ppermute | solution.py:260
  48.2 8.4 %collective-permute-start.3 = (bf16[288,128]{1,0:T(8,128)(2,1)S(1)}, bf16[288,128]{1,0:T(8,128)(2,1)S(1)}, u32[]{:S(2)}, u32[]{:S(2)}) collective-permute-start(bf16[288,128]{1,0:T(8,128)(2,1)S(1)} %get-tuple-element.23), channel_id=1, source_target_pairs={{1,2},{2,1},{3,4},{4,3},{5,6},{6,5},{7,8},{8,7},{9,10},{10,9},{11,... | collective-permute-start | bytes 221192 | tf_op jit(solution)/shard_map/ppermute | solution.py:259
  56.6 1.9 %copy-start = (bf16[4,256,1536]{2,1,0:T(8,128)(2,1)S(1)}, bf16[4,256,1536]{2,1,0:T(8,128)(2,1)}, u32[]{:S(2)}) copy-start(bf16[4,256,1536]{2,1,0:T(8,128)(2,1)} %get-tuple-element.25.table_x) | copy-start | bytes 9437188

commit v2 on v1

v2 whole, which is shorter than its diff:
```python
import jax
import jax.numpy as jnp
from jax import lax
from jax.experimental import pallas as pl
from jax.experimental.pallas import tpu as pltpu
from jax.sharding import PartitionSpec as P

step_rate = 0.05
PAD = 16
LANES = 128
CROSS = 32
NT = (((1,), (1,)), ((), ()))
NN = (((1,), (0,)), ((), ()))


def lookup(row, index):
    return jnp.take_along_axis(jnp.broadcast_to(row, index.shape), index, axis=1)


def grouped(value):
    out = []
    for j in range(value.shape[0] // 4):
        total = value[4 * j]
        for i in range(1, 4):
            total = total + pltpu.roll(value[4 * j + i], CROSS * i, axis=1)
        out.append(total)
    return out


def place(dst, src, first, count, tile_of, offset, lanes):
    for i in range(count):
        here = [tile_of == first + i - j for j in range(3)]
        for k in range(lanes // LANES):
            cut = pl.ds(k * LANES, LANES)
            value = jnp.zeros((PAD, LANES), jnp.bfloat16)
            for j in range(3):
                value = jnp.where(here[j], src[pl.ds(PAD * j, PAD), cut], value)
            dst[pl.ds(offset + PAD * i, PAD), cut] = value


def tiles_of(centre):
    return jnp.broadcast_to((centre + 1) // PAD, (PAD, LANES)).astype(jnp.bfloat16)


def spread(value, lane):
    first = jnp.where(lane < CROSS, value, 0)
    out = first
    for i in range(1, 4):
        out = out + pltpu.roll(first, CROSS * i, axis=1)
    return out


def starts(scalars, height):
    even = scalars[0] == 0
    start_a = pl.multiple_of(jnp.where(even, height, 0), 2 * PAD)
    start_b = pl.multiple_of(jnp.where(even, 0, height), 2 * PAD)
    return start_a, start_b


def strip_kernel(
    scalars, pos_hbm, amp_hbm, psf_rows_hbm, psf_cols_hbm, image_hbm,
    send, fine_y, fine_scaled, table_x, cross_fine_y, cross_fine_scaled, cross_x,
    pos, amp, psf_rows, psf_cols, image, sems, tmpl_y, tmpl_x, flux, fine_x, strip, cross_strip, cross_fine_x,
):
    comps, bands, taps = psf_rows.shape
    width = table_x.shape[1]
    height = width
    start_b = starts(scalars, height)[1]
    top = scalars[0] == 0
    image_row = pl.multiple_of(jnp.where(top, 0, height - PAD), PAD)
    copies = [
        pltpu.make_async_copy(pos_hbm, pos, sems.at[0]),
        pltpu.make_async_copy(psf_cols_hbm, psf_cols, sems.at[1]),
        pltpu.make_async_copy(psf_rows_hbm, psf_rows, sems.at[2]),
        pltpu.make_async_copy(amp_hbm, amp, sems.at[3]),
        pltpu.make_async_copy(image_hbm.at[:, pl.ds(image_row, PAD), :], image, sems.at[4]),
    ]
    for copy in copies:
        copy.start()
    live = scalars[2]
    lane = lax.broadcasted_iota(jnp.int32, (1, LANES), 1)
    base = (lane // CROSS) * CROSS
    tmpl_y[...] = jnp.zeros_like(tmpl_y)
    tmpl_x[...] = jnp.zeros_like(tmpl_x)
    cross_x[...] = jnp.zeros_like(cross_x)
    for copy in copies[:4]:
        copy.wait()
    tmpl_y[:, :, :taps] = psf_rows[...].astype(jnp.float32)
    tmpl_x[:, :, :taps] = psf_cols[...].astype(jnp.float32)
    flux[...] = jnp.where(lane < live, amp[...], 0.0)
    row, col = pos[0:1, :], pos[1:2, :]
    inner = lax.broadcasted_iota(jnp.int32, (3 * PAD, LANES), 0)

    def fine_index(centre, outside, add):
        tap = inner - (centre + 1) % PAD
        return jnp.where((tap >= 0) & (tap < taps), tap, outside) + add

    index_y, index_x = fine_index(row, LANES - 1, 0), fine_index(col, LANES - 1, 0)
    tile_y, tile_x = tiles_of(row), tiles_of(col)
    row_four, col_four = spread(row, lane), spread(col, lane)
    cross_index_y, cross_index_x = fine_index(row_four, CROSS - 1, base), fine_index(col_four, CROSS - 1, base)
    cross_tile_y, cross_tile_x = tiles_of(row_four), tiles_of(col_four)
    first_tile = start_b // PAD

    def tile_in_strip(i, j, tile):
        return tile == (first_tile + (i - j)).astype(jnp.bfloat16)

    def one_band(b, carry):
        for k in range(comps):
            cut = pl.ds(k * LANES, LANES)
            placed = lookup(tmpl_y[k, pl.ds(b, 1), :], index_y)
            fine_y[b, :, cut] = placed.astype(jnp.bfloat16)
            fine_scaled[b, :, cut] = (placed * flux[k, pl.ds(b, 1), :]).astype(jnp.bfloat16)
            fine_x[:, cut] = lookup(tmpl_x[k, pl.ds(b, 1), :], index_x).astype(jnp.bfloat16)
        place(table_x.at[b], fine_x, 1, width // PAD, tile_x, 0, comps * LANES)
        for i in range(2):
            for k in range(comps):
                cut = pl.ds(k * LANES, LANES)
                value = jnp.zeros((PAD, LANES), jnp.bfloat16)
                for j in range(3):
                    value = jnp.where(tile_in_strip(i, j, tile_y), fine_scaled[b, pl.ds(PAD * j, PAD), cut], value)
                strip[pl.ds(PAD * i, PAD), cut] = value
        model = lax.dot_general(strip[...], table_x[b], NT, preferred_element_type=jnp.float32)
        send[pl.ds(b * 2 * PAD, 2 * PAD), :] = (-model).astype(jnp.bfloat16)
        shown = image[b].astype(jnp.float32)
        mine = jnp.where(top, model[PAD:], model[:PAD])
        row_at = pl.multiple_of(b * 2 * PAD + jnp.where(top, PAD, 0), PAD)
        send[pl.ds(row_at, PAD), :] = (shown - mine).astype(jnp.bfloat16)
        return carry

    copies[4].wait()
    lax.fori_loop(0, bands, one_band, 0)

    four_y = grouped(tmpl_y[...])
    four_x = grouped(tmpl_x[...])
    four_flux = grouped(jnp.where(lane < CROSS, flux[...], 0.0))
    for b in range(bands):
        for j in range(comps // 4):
            cut = pl.ds((b * (comps // 4) + j) * LANES, LANES)
            placed = lookup(four_y[j][b : b + 1], cross_index_y)
            cross_fine_y[:, cut] = placed.astype(jnp.bfloat16)
            cross_fine_scaled[:, cut] = (placed * four_flux[j][b : b + 1]).astype(jnp.bfloat16)
            cross_fine_x[:, cut] = lookup(four_x[j][b : b + 1], cross_index_x).astype(jnp.bfloat16)
            for side_at, tile in ((0, 0), (PAD, width // PAD + 1)):
                value = jnp.zeros((PAD, LANES), jnp.bfloat16)
                for p in range(3):
                    value = jnp.where(cross_tile_x == tile - p, cross_fine_x[pl.ds(PAD * p, PAD), cut], value)
                cross_x[pl.ds(b * CROSS + side_at, PAD), cut] = value
            for i in range(2):
                value = jnp.zeros((PAD, LANES), jnp.bfloat16)
                for p in range(3):
                    value = jnp.where(tile_in_strip(i, p, cross_tile_y), cross_fine_scaled[pl.ds(PAD * p, PAD), cut], value)
                cross_strip[pl.ds(PAD * i, PAD), cut] = value
    wide = -lax.dot_general(cross_strip[...], cross_x[...], NT, preferred_element_type=jnp.float32)
    send[pl.ds(bands * 2 * PAD, PAD), pl.ds(0, LANES)] = wide[:PAD].astype(jnp.bfloat16)
    send[pl.ds(bands * 2 * PAD, PAD), pl.ds(LANES, LANES)] = wide[PAD:].astype(jnp.bfloat16)


def render_kernel(
    scalars, pos, image, fine_y, fine_scaled, table_x, cross_fine_y, cross_fine_scaled, cross_x,
    field, side, send, table_y, cross_y, scaled, cross_scaled,
):
    bands, ext, width = field.shape
    height = ext - 2 * PAD
    lane = lax.broadcasted_iota(jnp.int32, (1, LANES), 1)
    row = pos[0:1, :]
    tile_y = tiles_of(row)
    cross_tile_y = tiles_of(spread(row, lane))

    def one_band(b, carry):
        place(scaled, fine_scaled.at[b], 0, ext // PAD, tile_y, 0, scaled.shape[1])
        model = lax.dot_general(scaled[...], table_x[b], NT, preferred_element_type=jnp.float32)
        field[b] = -model
        field[b, pl.ds(PAD, height), :] += image[b].astype(jnp.float32)
        place(table_y.at[b], fine_y.at[b], 0, ext // PAD, tile_y, 0, scaled.shape[1])
        return carry

    lax.fori_loop(0, bands, one_band, 0)
    place(cross_scaled, cross_fine_scaled, 0, ext // PAD, cross_tile_y, 0, cross_scaled.shape[1])
    place(cross_y, cross_fine_y, 0, ext // PAD, cross_tile_y, 0, cross_scaled.shape[1])
    side[...] = -lax.dot_general(cross_scaled[...], cross_x[...], NT, preferred_element_type=jnp.float32)
    start = starts(scalars, height)[0]
    for b in range(bands):
        send[pl.ds(b * 2 * PAD, 2 * PAD), :] = field[b, pl.ds(start, 2 * PAD), :].astype(jnp.bfloat16)
    wide = side[pl.ds(start, 2 * PAD), :].astype(jnp.bfloat16)
    send[pl.ds(bands * 2 * PAD, PAD), pl.ds(0, LANES)] = wide[:PAD]
    send[pl.ds(bands * 2 * PAD, PAD), pl.ds(LANES, LANES)] = wide[PAD:]


def add_rows(scalars, field, side, got_a, got_b):
    bands, ext = field.shape[0], field.shape[1]
    height = ext - 2 * PAD
    start_a, start_b = starts(scalars, height)
    for got, start in ((got_a, start_a), (got_b, start_b)):
        for b in range(bands):
            field[b, pl.ds(start, 2 * PAD), :] += got[pl.ds(b * 2 * PAD, 2 * PAD), :].astype(jnp.float32)
        side[pl.ds(start, PAD), :] += got[pl.ds(bands * 2 * PAD, PAD), pl.ds(0, LANES)].astype(jnp.float32)
        side[pl.ds(start + PAD, PAD), :] += got[pl.ds(bands * 2 * PAD, PAD), pl.ds(LANES, LANES)].astype(jnp.float32)


def column_kernel(scalars, field_in, side_in, got_a, got_b, field, side, send_a, send_b):
    bands, ext, width = field.shape
    field[...] = field_in[...]
    side[...] = side_in[...]
    add_rows(scalars, field, side, got_a, got_b)
    even = scalars[1] == 0
    lane = lax.broadcasted_iota(jnp.int32, (1, LANES), 1)
    to_left = side[...]
    to_right = side[...]
    for b in range(bands):
        low = pltpu.roll(field[b, :, pl.ds(0, LANES)], CROSS * b + PAD, axis=1)
        to_left = jnp.where((lane >= CROSS * b + PAD) & (lane < CROSS * (b + 1)), low, to_left)
        high = pltpu.roll(field[b, :, pl.ds(width - LANES, LANES)], CROSS * b + PAD, axis=1)
        to_right = jnp.where((lane >= CROSS * b) & (lane < CROSS * b + PAD), high, to_right)
    send_a[...] = jnp.where(even, to_right, to_left).astype(jnp.bfloat16)
    send_b[...] = jnp.where(even, to_left, to_right).astype(jnp.bfloat16)


def gradient_kernel(
    scalars, amp, field, side, got_a, got_b, table_y, table_x, cross_y, cross_x,
    updated, residual, total, gradient, sem,
):
    bands, ext, width = field.shape
    height = ext - 2 * PAD
    comps = amp.shape[0]
    even = scalars[1] == 0
    live = scalars[2]
    lane = lax.broadcasted_iota(jnp.int32, (1, LANES), 1)
    from_a, from_b = got_a[...].astype(jnp.float32), got_b[...].astype(jnp.float32)
    from_left = jnp.where(even, from_b, from_a)
    from_right = jnp.where(even, from_a, from_b)
    total[...] = field[...]
    for b in range(bands):
        low = pltpu.roll(from_left, LANES - CROSS * b - PAD, axis=1)
        total[b, :, pl.ds(0, LANES)] += jnp.where(lane < PAD, low, 0.0)
        high = pltpu.roll(from_right, LANES - CROSS * b - PAD, axis=1)
        total[b, :, pl.ds(width - LANES, LANES)] += jnp.where(lane >= LANES - PAD, high, 0.0)
    outer = side[...] + jnp.where(lane % CROSS < PAD, from_left, from_right)
    low_row, high_row, low_col, high_col = scalars[3], scalars[4], scalars[5], scalars[6]
    pixel_y = lax.broadcasted_iota(jnp.int32, (ext, LANES), 0)
    inside = (pixel_y >= low_row) & (pixel_y < high_row)
    inside = inside & (lane % CROSS >= low_col) & (lane % CROSS < high_col)
    outer = jnp.where(inside, outer, 0.0)

    @pl.when(low_row > 0)
    def _():
        total[:, pl.ds(0, PAD), :] = jnp.zeros((bands, PAD, width), jnp.float32)

    @pl.when(high_row < ext)
    def _():
        total[:, pl.ds(ext - PAD, PAD), :] = jnp.zeros((bands, PAD, width), jnp.float32)

    leaving = pltpu.make_async_copy(total.at[:, pl.ds(PAD, height), :], residual, sem)
    leaving.start()

    def one_band(b, carry):
        rounded = total[b].astype(jnp.bfloat16)
        for k in range(0, comps, 2):
            cut = pl.ds(k * LANES, 2 * LANES)
            inner = lax.dot_general(rounded, table_x[b, :, cut], NN, preferred_element_type=jnp.float32)
            summed = jnp.sum(inner * table_y[b, :, cut].astype(jnp.float32), axis=0, keepdims=True)
            gradient[k, pl.ds(b, 1), :] = summed[:, :LANES]
            gradient[k + 1, pl.ds(b, 1), :] = summed[:, LANES:]
        return carry

    lax.fori_loop(0, bands, one_band, 0)

    inner = lax.dot_general(outer.astype(jnp.bfloat16), cross_x[...], NN, preferred_element_type=jnp.float32)
    summed = jnp.sum(inner * cross_y[...].astype(jnp.float32), axis=0, keepdims=True)
    for b in range(bands):
        for j in range(comps // 4):
            start = (b * (comps // 4) + j) * LANES
            four = summed[:, start : start + LANES]
            for i in range(4):
                part = four if i == 0 else pltpu.roll(four, LANES - CROSS * i, axis=1)
                gradient[4 * j + i, b : b + 1, :] += jnp.where(lane < CROSS, part, 0.0)
    updated[...] = amp[...] + step_rate * jnp.where(lane < live, gradient[...], 0.0)
    leaving.wait()


SMEM = pl.BlockSpec(memory_space=pltpu.SMEM)
VMEM = pl.BlockSpec(memory_space=pltpu.VMEM)
HBM = pl.BlockSpec(memory_space=pltpu.HBM)
params = pltpu.CompilerParams(vmem_limit_bytes=16 << 20)


def swaps(axis, first):
    out = []
    for i in range(first, lax.axis_size(axis) - 1, 2):
        out += [(i, i + 1), (i + 1, i)]
    return out


def on_device(image, amplitude, positions, live, psf_rows, psf_cols):
    amp = jnp.swapaxes(amplitude[0, 0], 0, 1)
    psf_rows, psf_cols = jnp.swapaxes(psf_rows, 0, 1), jnp.swapaxes(psf_cols, 0, 1)
    bands, height, width = image.shape
    comps, slots = amp.shape[0], amp.shape[2]
    ext = height + 2 * PAD
    shape = jax.ShapeDtypeStruct
    f32, bf16 = jnp.float32, jnp.bfloat16
    region, tile = lax.axis_index("region"), lax.axis_index("tile")
    scalars = jnp.stack([
        region % 2,
        tile % 2,
        live[0, 0],
        jnp.where(region == 0, PAD, 0),
        jnp.where(region == lax.axis_size("region") - 1, ext - PAD, ext),
        jnp.where(tile == 0, PAD, 0),
        jnp.where(tile == lax.axis_size("tile") - 1, PAD, 2 * PAD),
    ]).astype(jnp.int32)
    rows_sent = bands * 2 * PAD + PAD
    table_width = comps * slots
    fine = shape((bands, 3 * PAD, table_width), bf16)
    cross_width = bands * comps * CROSS
    cross_fine = shape((3 * PAD, cross_width), bf16)
    centres = positions[:, 0, 0]
    send_b, fine_y, fine_scaled, table_x, cross_fine_y, cross_fine_scaled, cross_x = pl.pallas_call(
        strip_kernel,
        out_shape=[
            shape((rows_sent, width), bf16), fine, fine, shape((bands, width, table_width), bf16),
            cross_fine, cross_fine, shape((bands * CROSS, cross_width), bf16),
        ],
        in_specs=[SMEM] + [HBM] * 5,
        out_specs=[VMEM] * 7,
        scratch_shapes=[
            pltpu.VMEM(centres.shape, jnp.int32), pltpu.VMEM(amp.shape, f32),
            pltpu.VMEM(psf_rows.shape, bf16), pltpu.VMEM(psf_cols.shape, bf16),
            pltpu.VMEM((bands, PAD, width), bf16), pltpu.SemaphoreType.DMA((5,)),
            pltpu.VMEM((comps, bands, LANES), f32), pltpu.VMEM((comps, bands, LANES), f32),
            pltpu.VMEM((comps, bands, LANES), f32), pltpu.VMEM((3 * PAD, table_width), bf16),
            pltpu.VMEM((2 * PAD, table_width), bf16), pltpu.VMEM((2 * PAD, cross_width), bf16),
            pltpu.VMEM((3 * PAD, cross_width), bf16),
        ],
        compiler_params=params,
    )(scalars, *[pltpu.with_memory_space_constraint(x, pltpu.HBM) for x in (centres, amp, psf_rows, psf_cols, image)])
    got_b = lax.ppermute(send_b, "region", swaps("region", 1))
    field, side, send_a, table_y, cross_y = pl.pallas_call(
        render_kernel,
        out_shape=[
            shape((bands, ext, width), f32), shape((ext, LANES), f32), shape((rows_sent, width), bf16),
            shape((bands, ext, table_width), bf16), shape((ext, cross_width), bf16),
        ],
        in_specs=[SMEM] + [VMEM] * 8,
        out_specs=[VMEM] * 5,
        scratch_shapes=[pltpu.VMEM((ext, table_width), bf16), pltpu.VMEM((ext, cross_width), bf16)],
        compiler_params=params,
    )(scalars, centres, image, fine_y, fine_scaled, table_x, cross_fine_y, cross_fine_scaled, cross_x)
    got_a = lax.ppermute(send_a, "region", swaps("region", 0))
    field, side, send_a, send_b = pl.pallas_call(
        column_kernel,
        out_shape=[
            shape((bands, ext, width), f32), shape((ext, LANES), f32),
            shape((ext, LANES), bf16), shape((ext, LANES), bf16),
        ],
        in_specs=[SMEM] + [VMEM] * 4,
        out_specs=[VMEM] * 4,
        compiler_params=params,
    )(scalars, field, side, got_a, got_b)
    got_b = lax.ppermute(send_b, "tile", swaps("tile", 1))
    got_a = lax.ppermute(send_a, "tile", swaps("tile", 0))
    updated, residual = pl.pallas_call(
        gradient_kernel,
        out_shape=[shape(amp.shape, f32), shape(image.shape, f32)],
        in_specs=[SMEM] + [VMEM] * 9,
        out_specs=[VMEM, HBM],
        scratch_shapes=[
            pltpu.VMEM((bands, ext, width), f32), pltpu.VMEM((comps, bands, LANES), f32),
            pltpu.SemaphoreType.DMA,
        ],
        compiler_params=params,
    )(scalars, amp, field, side, got_a, got_b, table_y, table_x, cross_y, cross_x)
    return (jnp.swapaxes(updated, 0, 1)[None, None], residual)


def solution(mesh):
    in_specs = (
        P(None, "region", "tile"),
        P("region", "tile", None, None, None),
        P(None, "region", "tile", None),
        P("region", "tile"),
        P(),
        P(),
    )
    out_specs = (P("region", "tile", None, None, None), P(None, "region", "tile"))
    return jax.shard_map(
        on_device, mesh=mesh, in_specs=in_specs, out_specs=out_specs, check_vma=False
    )
```

time: 64.1 us -> 45.7 us (0.71)
  the two profiles are of different devices: /device:TPU:56 before, /device:TPU:6 now
where the time goes in v2:
time: 45.7 us; the launch traced here: 45.4 us
  starting transfers between devices  24 us (53%)
  Pallas kernels  12.5 us (27%)
  waiting for transfers between devices  5.73 us (13%)
  local copies, waits for them, and re-layouts  1.81 us (4%)
  between operations  1.38 us (3%)
    ppermute x1, starting transfers between devices, on_device(): got_a = lax.ppermute(send_a, 'region', swaps('region', 0))  17.1 us
    ppermute x1, waiting for transfers between devices, on_device(): got_b = lax.ppermute(send_b, 'tile', swaps('tile', 1))  4.68 us
    pallas_call x1, Pallas kernels, on_device(): pl.pallas_call(strip_kernel, out_shape=[shape((rows_sent, width), bf16),...  4.36 us
    pallas_call x1, Pallas kernels, on_device(): pl.pallas_call(render_kernel, out_shape=[shape((bands, ext, width), f32),...  3.71 us
    ppermute x1, starting transfers between devices, on_device(): got_b = lax.ppermute(send_b, 'tile', swaps('tile', 1))  3.5 us
    pallas_call x1, Pallas kernels, on_device(): pl.pallas_call(gradient_kernel, out_shape=[shape(amp.shape, f32), shape(i...  3.5 us
    ppermute x1, starting transfers between devices, on_device(): got_a = lax.ppermute(send_a, 'tile', swaps('tile', 0))  2.74 us
    unnamed x6, local copies, waits for them, and re-layouts  1.72 us
  transfers between devices with their start and end apart: 4, of which 3 were waited for; matrix products, arithmetic and copies ran while one was open for 0% of the time, Pallas kernels for 8%

profile of v2, /device:TPU:6, one launch (start us, length us, event | category | flops | bytes accessed | tf_op | source)
XLA Modules:
  0.0 45.4 jit_solution(6049277084688519855)
XLA Ops:
  1.3 0.1 stack.27.scalars
  1.4 4.4 %shard_map.77 = (bf16[144,256]{1,0:T(8,128)(2,1)S(1)}, bf16[4,48,1536]{2,1,0:T(8,128)(2,1)S(1)}, bf16[4,48,1536]{2,1,0:T(8,128)(2,1)S(1)}, bf16[4,256,1536]{2,1,...) custom-call(s32[7]{0:T(128)S(1)} %stack.27.scalars, ...), custom_call_target="tpu_custom_call" | custom-call | tf_op jit(solution)/shard_map/pallas_call | solution.py:318
  5.8 0.7 %collective-permute-start.1 = (bf16[144,256]{1,0:T(8,128)(2,1)S(1)}, bf16[144,256]{1,0:T(8,128)(2,1)S(1)}, u32[]{:S(2)}, u32[]{:S(2)}) collective-permute-start(bf16[144,256]{1,0:T(8,128)(2,1)S(1)} %get-tuple-element.29), channel_id=1, source_target_pairs={{32,64},{64,32},{96,128},{128,96},{160,192},{192,160},{224,256},{2... | collective-permute-start | bytes 221192 | tf_op jit(solution)/shard_map/ppermute | solution.py:337
  6.4 0.0 copy-start
  6.5 1.0 %copy-done = bf16[4,256,256]{2,1,0:T(8,128)(2,1)S(1)} copy-done((bf16[4,256,256]{2,1,0:T(8,128)(2,1)S(1)}, bf16[4,256,256]{2,1,0:T(8,128)(2,1)}, u32[]{:S(2)}) %copy-start) | copy-done | bytes 524312
  7.5 0.0 copy-start.2
  7.5 0.7 %copy-done.2 = s32[2,1,1,128]{3,2,1,0:T(1,128)S(1)} copy-done((s32[2,1,1,128]{3,2,1,0:T(1,128)S(1)}, s32[2,1,1,128]{3,2,1,0:T(1,128)}, u32[]{:S(2)}) %copy-start.2) | copy-done | bytes 1048
  8.2 0.0 copy-start.1
  8.2 3.7 %shard_map.78 = (f32[4,288,256]{2,1,0:T(8,128)S(1)}, f32[288,128]{1,0:T(8,128)S(1)}, bf16[144,256]{1,0:T(8,128)(2,1)S(1)}, bf16[4,288,1536]{2,1,0:T(8,128)(2,1)S(1)}, bf16[288,1536]{1,0:T(8,128)(2,1)S(1)}) custom-call(s32[7]{0:T(128)S(1)} %stack.27.scalars, s32[2,128]{1,0:T(2,128)S(1)} %bitcast.20, bf16[4,256,256]{2,1,0:T(8,128)(2,1)S(1)} %copy-done, ...), custom_call_target="tpu_custom_call" | custom-call | tf_op jit(solution)/shard_map/pallas_call | solution.py:338
  11.9 17.1 %collective-permute-start = (bf16[144,256]{1,0:T(8,128)(2,1)S(1)}, bf16[144,256]{1,0:T(8,128)(2,1)S(1)}, u32[]{:S(2)}, u32[]{:S(2)}) collective-permute-start(bf16[144,256]{1,0:T(8,128)(2,1)S(1)} %get-tuple-element.28), channel_id=1, source_target_pairs={{0,32},{32,0},{64,96},{96,64},{128,160},{160,128},{192,224},{224,1... | collective-permute-start | bytes 221192 | tf_op jit(solution)/shard_map/ppermute | solution.py:349
  29.0 0.0 collective-permute-done.1.got_b
  29.0 0.9 %collective-permute-done.got_a = bf16[144,256]{1,0:T(8,128)(2,1)S(1)} collective-permute-done((bf16[144,256]{1,0:T(8,128)(2,1)S(1)}, bf16[144,256]{1,0:T(8,128)(2,1)S(1)}, u32[]{:S(2)}, u32[]{:S(2)}) %collective-permute-start) | collective-permute-done | bytes 73760 | tf_op jit(solution)/shard_map/ppermute | solution.py:349
  29.9 0.9 %shard_map.79 = (f32[4,288,256]{2,1,0:T(8,128)S(1)}, f32[288,128]{1,0:T(8,128)S(1)}, bf16[288,128]{1,0:T(8,128)(2,1)S(1)}, bf16[288,128]{1,0:T(8,128)(2,1)S(1)}) custom-call(s32[7]{0:T(128)S(1)} %stack.27.scalars, f32[4,288,256]{2,1,0:T(8,128)S(1)} %get-tuple-element.26.field_in, f32[288,128]{1,0:T(8,128)S(1)} %get-tuple-element.27.side_in, ...), custom_call_target="tpu_custom_call" | custom-call | tf_op jit(solution)/shard_map/pallas_call | solution.py:350
  30.8 2.7 %collective-permute-start.2 = (bf16[288,128]{1,0:T(8,128)(2,1)S(1)}, bf16[288,128]{1,0:T(8,128)(2,1)S(1)}, u32[]{:S(2)}, u32[]{:S(2)}) collective-permute-start(bf16[288,128]{1,0:T(8,128)(2,1)S(1)} %get-tuple-element.32), channel_id=1, source_target_pairs={{0,1},{1,0},{2,3},{3,2},{4,5},{5,4},{6,7},{7,6},{8,9},{9,8},{10,11... | collective-permute-start | bytes 221192 | tf_op jit(solution)/shard_map/ppermute | solution.py:361
  33.5 3.5 %collective-permute-start.3 = (bf16[288,128]{1,0:T(8,128)(2,1)S(1)}, bf16[288,128]{1,0:T(8,128)(2,1)S(1)}, u32[]{:S(2)}, u32[]{:S(2)}) collective-permute-start(bf16[288,128]{1,0:T(8,128)(2,1)S(1)} %get-tuple-element.33), channel_id=1, source_target_pairs={{1,2},{2,1},{3,4},{4,3},{5,6},{6,5},{7,8},{8,7},{9,10},{10,9},{11,... | collective-permute-start | bytes 221192 | tf_op jit(solution)/shard_map/ppermute | solution.py:360
  37.0 0.2 collective-permute-done.2.got_a
  37.2 4.7 %collective-permute-done.3.got_b = bf16[288,128]{1,0:T(8,128)(2,1)S(1)} collective-permute-done((bf16[288,128]{1,0:T(8,128)(2,1)S(1)}, bf16[288,128]{1,0:T(8,128)(2,1)S(1)}, u32[]{:S(2)}, u32[]{:S(2)}) %collective-permute-start.3) | collective-permute-done | bytes 73760 | tf_op jit(solution)/shard_map/ppermute | solution.py:360
  41.9 0.0 copy-done.1
  41.9 3.5 %shard_map.80 = (f32[12,4,128]{2,1,0:T(4,128)}, f32[4,256,256]{2,1,0:T(8,128)}) custom-call(s32[7]{0:T(128)S(1)} %stack.27.scalars, f32[12,4,128]{2,1,0:T(4,128)S(1)} %bitcast.18, f32[4,288,256]{2,1,0:T(8,128)S(1)} %get-tuple-element.30.field, f32[288,128]{1,0:T(8,128)S(1)} %get-tuple-element.31.side, bf16[288,128]{1,0:T(8,128)(2,1)S(1)} %collective-permute-done.2.got_a, ...), custom_call_target="tpu_custom_call" | custom-call | tf_op jit(solution)/shard_map/pallas_call | solution.py:362
Async XLA Ops:
  5.8 23.2 %collective-permute-start.1 = (bf16[144,256]{1,0:T(8,128)(2,1)S(1)}, bf16[144,256]{1,0:T(8,128)(2,1)S(1)}, u32[]{:S(2)}, u32[]{:S(2)}) collective-permute-start(bf16[144,256]{1,0:T(8,128)(2,1)S(1)} %get-tuple-element.29), channel_id=1, source_target_pairs={{32,64},{64,32},{96,128},{128,96},{160,192},{192,160},{224,256},{2... | collective-permute-start | bytes 221192 | tf_op jit(solution)/shard_map/ppermute | solution.py:337
  6.4 1.0 %copy-start = (bf16[4,256,256]{2,1,0:T(8,128)(2,1)S(1)}, bf16[4,256,256]{2,1,0:T(8,128)(2,1)}, u32[]{:S(2)}) copy-start(bf16[4,256,256]{2,1,0:T(8,128)(2,1)} %image.1) | copy-start | bytes 1572868
  7.5 0.7 %copy-start.2 = (s32[2,1,1,128]{3,2,1,0:T(1,128)S(1)}, s32[2,1,1,128]{3,2,1,0:T(1,128)}, u32[]{:S(2)}) copy-start(s32[2,1,1,128]{3,2,1,0:T(1,128)} %param.8) | copy-start | bytes 3076
  8.2 33.7 %copy-start.1 = (f32[1,1,4,12,128]{4,2,3,1,0:T(4,128)S(1)}, f32[1,1,4,12,128]{4,2,3,1,0:T(4,128)}, u32[]{:S(2)}) copy-start(f32[1,1,4,12,128]{4,2,3,1,0:T(4,128)} %param.7) | copy-start | bytes 73732
  11.9 18.0 %collective-permute-start = (bf16[144,256]{1,0:T(8,128)(2,1)S(1)}, bf16[144,256]{1,0:T(8,128)(2,1)S(1)}, u32[]{:S(2)}, u32[]{:S(2)}) collective-permute-start(bf16[144,256]{1,0:T(8,128)(2,1)S(1)} %get-tuple-element.28), channel_id=1, source_target_pairs={{0,32},{32,0},{64,96},{96,64},{128,160},{160,128},{192,224},{224,1... | collective-permute-start | bytes 221192 | tf_op jit(solution)/shard_map/ppermute | solution.py:349
  30.8 6.4 %collective-permute-start.2 = (bf16[288,128]{1,0:T(8,128)(2,1)S(1)}, bf16[288,128]{1,0:T(8,128)(2,1)S(1)}, u32[]{:S(2)}, u32[]{:S(2)}) collective-permute-start(bf16[288,128]{1,0:T(8,128)(2,1)S(1)} %get-tuple-element.32), channel_id=1, source_target_pairs={{0,1},{1,0},{2,3},{3,2},{4,5},{5,4},{6,7},{7,6},{8,9},{9,8},{10,11... | collective-permute-start | bytes 221192 | tf_op jit(solution)/shard_map/ppermute | solution.py:361
  33.5 8.4 %collective-permute-start.3 = (bf16[288,128]{1,0:T(8,128)(2,1)S(1)}, bf16[288,128]{1,0:T(8,128)(2,1)S(1)}, u32[]{:S(2)}, u32[]{:S(2)}) collective-permute-start(bf16[288,128]{1,0:T(8,128)(2,1)S(1)} %get-tuple-element.33), channel_id=1, source_target_pairs={{1,2},{2,1},{3,4},{4,3},{5,6},{6,5},{7,8},{8,7},{9,10},{10,9},{11,... | collective-permute-start | bytes 221192 | tf_op jit(solution)/shard_map/ppermute | solution.py:360

commit v3 on v2

v3 whole, which is shorter than its diff:
```python
import jax
import jax.numpy as jnp
from jax import lax
from jax.experimental import pallas as pl
from jax.experimental.pallas import tpu as pltpu
from jax.sharding import PartitionSpec as P

step_rate = 0.05
PAD = 16
LANES = 128
CROSS = 32
NT = (((1,), (1,)), ((), ()))
NN = (((1,), (0,)), ((), ()))


def lookup(row, index):
    return jnp.take_along_axis(jnp.broadcast_to(row, index.shape), index, axis=1)


def grouped(value):
    out = []
    for j in range(value.shape[0] // 4):
        total = value[4 * j]
        for i in range(1, 4):
            total = total + pltpu.roll(value[4 * j + i], CROSS * i, axis=1)
        out.append(total)
    return out


def place(dst, src, first, count, tile_of, offset, lanes):
    for i in range(count):
        here = [tile_of == first + i - j for j in range(3)]
        for k in range(lanes // LANES):
            cut = pl.ds(k * LANES, LANES)
            value = jnp.zeros((PAD, LANES), jnp.bfloat16)
            for j in range(3):
                value = jnp.where(here[j], src[pl.ds(PAD * j, PAD), cut], value)
            dst[pl.ds(offset + PAD * i, PAD), cut] = value


def tiles_of(centre):
    return jnp.broadcast_to((centre + 1) // PAD, (PAD, LANES)).astype(jnp.bfloat16)


def spread(value, lane):
    first = jnp.where(lane < CROSS, value, 0)
    out = first
    for i in range(1, 4):
        out = out + pltpu.roll(first, CROSS * i, axis=1)
    return out


def starts(scalars, height):
    even = scalars[0] == 0
    start_a = pl.multiple_of(jnp.where(even, height, 0), 2 * PAD)
    start_b = pl.multiple_of(jnp.where(even, 0, height), 2 * PAD)
    return start_a, start_b


def sides(scalars, got_a, got_b):
    even = scalars[1] == 0
    from_a, from_b = got_a.astype(jnp.float32), got_b.astype(jnp.float32)
    return jnp.where(even, from_b, from_a), jnp.where(even, from_a, from_b)


def low_columns(from_left, b, lane):
    return jnp.where(lane < PAD, pltpu.roll(from_left, LANES - CROSS * b - PAD, axis=1), 0.0)


def high_columns(from_right, b, lane):
    return jnp.where(lane >= LANES - PAD, pltpu.roll(from_right, LANES - CROSS * b - PAD, axis=1), 0.0)


def render_kernel(
    scalars, pos_hbm, amp_hbm, psf_rows_hbm, psf_cols_hbm, image_hbm,
    send_a, send_b, field, side, fine_y, table_x, cross_fine_y, cross_x, tiles, amp,
    pos, psf_rows, psf_cols, image, sems, tmpl_y, tmpl_x, flux,
    fine_scaled, fine_x, scaled, cross_fine_scaled, cross_fine_x, cross_scaled,
):
    comps, bands, taps = psf_rows.shape
    ext, width = field.shape[1], field.shape[2]
    height = ext - 2 * PAD
    copies = [
        pltpu.make_async_copy(pos_hbm, pos, sems.at[0]),
        pltpu.make_async_copy(psf_cols_hbm, psf_cols, sems.at[1]),
        pltpu.make_async_copy(psf_rows_hbm, psf_rows, sems.at[2]),
        pltpu.make_async_copy(amp_hbm, amp, sems.at[3]),
        pltpu.make_async_copy(image_hbm, image, sems.at[4]),
    ]
    for copy in copies:
        copy.start()
    live = scalars[2]
    lane = lax.broadcasted_iota(jnp.int32, (1, LANES), 1)
    base = (lane // CROSS) * CROSS
    tmpl_y[...] = jnp.zeros_like(tmpl_y)
    tmpl_x[...] = jnp.zeros_like(tmpl_x)
    cross_x[...] = jnp.zeros_like(cross_x)
    for copy in copies[:4]:
        copy.wait()
    tmpl_y[:, :, :taps] = psf_rows[...].astype(jnp.float32)
    tmpl_x[:, :, :taps] = psf_cols[...].astype(jnp.float32)
    flux[...] = jnp.where(lane < live, amp[...], 0.0)
    row, col = pos[0:1, :], pos[1:2, :]
    inner = lax.broadcasted_iota(jnp.int32, (3 * PAD, LANES), 0)

    def fine_index(centre, outside, add):
        tap = inner - (centre + 1) % PAD
        return jnp.where((tap >= 0) & (tap < taps), tap, outside) + add

    index_y, index_x = fine_index(row, LANES - 1, 0), fine_index(col, LANES - 1, 0)
    tile_y, tile_x = tiles_of(row), tiles_of(col)
    row_four, col_four = spread(row, lane), spread(col, lane)
    cross_index_y, cross_index_x = fine_index(row_four, CROSS - 1, base), fine_index(col_four, CROSS - 1, base)
    cross_tile_y, cross_tile_x = tiles_of(row_four), tiles_of(col_four)
    tiles[0] = tile_y
    tiles[1] = cross_tile_y

    four_y = grouped(tmpl_y[...])
    four_x = grouped(tmpl_x[...])
    four_flux = grouped(jnp.where(lane < CROSS, flux[...], 0.0))
    for b in range(bands):
        for j in range(comps // 4):
            cut = pl.ds((b * (comps // 4) + j) * LANES, LANES)
            placed = lookup(four_y[j][b : b + 1], cross_index_y)
            cross_fine_y[:, cut] = placed.astype(jnp.bfloat16)
            cross_fine_scaled[:, cut] = (placed * four_flux[j][b : b + 1]).astype(jnp.bfloat16)
            cross_fine_x[:, cut] = lookup(four_x[j][b : b + 1], cross_index_x).astype(jnp.bfloat16)
            for side_at, tile in ((0, 0), (PAD, width // PAD + 1)):
                value = jnp.zeros((PAD, LANES), jnp.bfloat16)
                for p in range(3):
                    value = jnp.where(cross_tile_x == tile - p, cross_fine_x[pl.ds(PAD * p, PAD), cut], value)
                cross_x[pl.ds(b * CROSS + side_at, PAD), cut] = value
    place(cross_scaled, cross_fine_scaled, 0, ext // PAD, cross_tile_y, 0, cross_scaled.shape[1])
    side[...] = -lax.dot_general(cross_scaled[...], cross_x[...], NT, preferred_element_type=jnp.float32)

    def one_band(b, buffers):
        fine_scaled, fine_x, scaled = buffers
        for k in range(comps):
            cut = pl.ds(k * LANES, LANES)
            placed = lookup(tmpl_y[k, pl.ds(b, 1), :], index_y)
            fine_y[b, :, cut] = placed.astype(jnp.bfloat16)
            fine_scaled[:, cut] = (placed * flux[k, pl.ds(b, 1), :]).astype(jnp.bfloat16)
            fine_x[:, cut] = lookup(tmpl_x[k, pl.ds(b, 1), :], index_x).astype(jnp.bfloat16)
        place(table_x.at[b], fine_x, 1, width // PAD, tile_x, 0, comps * LANES)
        place(scaled, fine_scaled, 0, ext // PAD, tile_y, 0, comps * LANES)
        field[b] = -lax.dot_general(scaled[...], table_x[b], NT, preferred_element_type=jnp.float32)

    for b in range(bands):
        one_band(b, (fine_scaled.at[b], fine_x.at[b], scaled.at[b]))
    copies[4].wait()
    for b in range(bands):
        field[b, pl.ds(PAD, height), :] += image[b].astype(jnp.float32)
    to_left = side[...]
    to_right = side[...]
    for b in range(bands):
        low = pltpu.roll(field[b, :, pl.ds(0, LANES)], CROSS * b + PAD, axis=1)
        to_left = jnp.where((lane >= CROSS * b + PAD) & (lane < CROSS * (b + 1)), low, to_left)
        high = pltpu.roll(field[b, :, pl.ds(width - LANES, LANES)], CROSS * b + PAD, axis=1)
        to_right = jnp.where((lane >= CROSS * b) & (lane < CROSS * b + PAD), high, to_right)
    even = scalars[1] == 0
    send_a[...] = jnp.where(even, to_right, to_left).astype(jnp.bfloat16)
    send_b[...] = jnp.where(even, to_left, to_right).astype(jnp.bfloat16)


def place_kernel(tiles, fine_y, cross_fine_y, ready, table_y, cross_y, send):
    bands, ext, columns = table_y.shape
    tile_y, cross_tile_y = tiles[0], tiles[1]

    def one_band(b, carry):
        place(table_y.at[b], fine_y.at[b], 0, ext // PAD, tile_y, 0, columns)
        return carry

    send[...] = ready[...]
    lax.fori_loop(0, bands, one_band, 0)
    place(cross_y, cross_fine_y, 0, ext // PAD, cross_tile_y, 0, cross_y.shape[1])


def strip_kernel(scalars, field, side, got_a, got_b, send_a, send_b):
    bands, ext, width = field.shape
    lane = lax.broadcasted_iota(jnp.int32, (1, LANES), 1)
    for send, start in zip((send_a, send_b), starts(scalars, ext - 2 * PAD)):
        rows = pl.ds(start, 2 * PAD)
        from_left, from_right = sides(scalars, got_a[rows, :], got_b[rows, :])
        for b in range(bands):
            to = pl.ds(b * 2 * PAD, 2 * PAD)
            low = field[b, rows, pl.ds(0, LANES)] + low_columns(from_left, b, lane)
            high = field[b, rows, pl.ds(width - LANES, LANES)] + high_columns(from_right, b, lane)
            send[to, pl.ds(0, LANES)] = low.astype(jnp.bfloat16)
            send[to, pl.ds(width - LANES, LANES)] = high.astype(jnp.bfloat16)
        wide = side[rows, :] + jnp.where(lane % CROSS < PAD, from_left, from_right)
        wide = wide.astype(jnp.bfloat16)
        send[pl.ds(bands * 2 * PAD, PAD), pl.ds(0, LANES)] = wide[:PAD]
        send[pl.ds(bands * 2 * PAD, PAD), pl.ds(LANES, LANES)] = wide[PAD:]


def gradient_kernel(
    scalars, amp, field, side, cols_a, cols_b, rows_a, rows_b, table_y, table_x, cross_y, cross_x,
    updated, residual, total, outer, gradient, sem,
):
    bands, ext, width = field.shape
    height = ext - 2 * PAD
    comps = amp.shape[0]
    live = scalars[2]
    lane = lax.broadcasted_iota(jnp.int32, (1, LANES), 1)
    from_left, from_right = sides(scalars, cols_a[...], cols_b[...])
    for b in range(bands):
        total[b, :, pl.ds(0, LANES)] = field[b, :, pl.ds(0, LANES)] + low_columns(from_left, b, lane)
        total[b, :, pl.ds(LANES, LANES)] = field[b, :, pl.ds(LANES, LANES)] + high_columns(from_right, b, lane)
    outer[...] = side[...] + jnp.where(lane % CROSS < PAD, from_left, from_right)
    for got, start in zip((rows_a, rows_b), starts(scalars, height)):
        for b in range(bands):
            total[b, pl.ds(start, 2 * PAD), :] += got[pl.ds(b * 2 * PAD, 2 * PAD), :].astype(jnp.float32)
        extra = pl.ds(bands * 2 * PAD, PAD)
        outer[pl.ds(start, PAD), :] += got[extra, pl.ds(0, LANES)].astype(jnp.float32)
        outer[pl.ds(start + PAD, PAD), :] += got[extra, pl.ds(LANES, LANES)].astype(jnp.float32)
    leaving = pltpu.make_async_copy(total.at[:, pl.ds(PAD, height), :], residual, sem)
    leaving.start()

    low_row, high_row, low_col, high_col = scalars[3], scalars[4], scalars[5], scalars[6]
    pixel_y = lax.broadcasted_iota(jnp.int32, (ext, LANES), 0)
    inside = (pixel_y >= low_row) & (pixel_y < high_row)
    inside = inside & (lane % CROSS >= low_col) & (lane % CROSS < high_col)
    beyond = jnp.where(inside, outer[...], 0.0).astype(jnp.bfloat16)

    @pl.when(low_row > 0)
    def _():
        total[:, pl.ds(0, PAD), :] = jnp.zeros((bands, PAD, width), jnp.float32)

    @pl.when(high_row < ext)
    def _():
        total[:, pl.ds(ext - PAD, PAD), :] = jnp.zeros((bands, PAD, width), jnp.float32)

    def one_band(b, carry):
        rounded = total[b].astype(jnp.bfloat16)
        for k in range(0, comps, 2):
            cut = pl.ds(k * LANES, 2 * LANES)
            inner = lax.dot_general(rounded, table_x[b, :, cut], NN, preferred_element_type=jnp.float32)
            summed = jnp.sum(inner * table_y[b, :, cut].astype(jnp.float32), axis=0, keepdims=True)
            gradient[k, pl.ds(b, 1), :] = summed[:, :LANES]
            gradient[k + 1, pl.ds(b, 1), :] = summed[:, LANES:]
        return carry

    lax.fori_loop(0, bands, one_band, 0)

    inner = lax.dot_general(beyond, cross_x[...], NN, preferred_element_type=jnp.float32)
    summed = jnp.sum(inner * cross_y[...].astype(jnp.float32), axis=0, keepdims=True)
    for b in range(bands):
        for j in range(comps // 4):
            start = (b * (comps // 4) + j) * LANES
            four = summed[:, start : start + LANES]
            for i in range(4):
                part = four if i == 0 else pltpu.roll(four, LANES - CROSS * i, axis=1)
                gradient[4 * j + i, b : b + 1, :] += jnp.where(lane < CROSS, part, 0.0)
    updated[...] = amp[...] + step_rate * jnp.where(lane < live, gradient[...], 0.0)
    leaving.wait()


SMEM = pl.BlockSpec(memory_space=pltpu.SMEM)
VMEM = pl.BlockSpec(memory_space=pltpu.VMEM)
HBM = pl.BlockSpec(memory_space=pltpu.HBM)
params = pltpu.CompilerParams(vmem_limit_bytes=16 << 20)


def swaps(axis, first):
    out = []
    for i in range(first, lax.axis_size(axis) - 1, 2):
        out += [(i, i + 1), (i + 1, i)]
    return out


def on_device(image, amplitude, positions, live, psf_rows, psf_cols):
    amp = jnp.swapaxes(amplitude[0, 0], 0, 1)
    psf_rows, psf_cols = jnp.swapaxes(psf_rows, 0, 1), jnp.swapaxes(psf_cols, 0, 1)
    bands, height, width = image.shape
    comps, slots = amp.shape[0], amp.shape[2]
    ext = height + 2 * PAD
    shape = jax.ShapeDtypeStruct
    f32, bf16 = jnp.float32, jnp.bfloat16
    region, tile = lax.axis_index("region"), lax.axis_index("tile")
    scalars = jnp.stack([
        region % 2,
        tile % 2,
        live[0, 0],
        jnp.where(region == 0, PAD, 0),
        jnp.where(region == lax.axis_size("region") - 1, ext - PAD, ext),
        jnp.where(tile == 0, PAD, 0),
        jnp.where(tile == lax.axis_size("tile") - 1, PAD, 2 * PAD),
    ]).astype(jnp.int32)
    rows_sent = bands * 2 * PAD + PAD
    table_width = comps * slots
    cross_width = bands * comps * CROSS
    centres = positions[:, 0, 0]
    strip = shape((ext, LANES), bf16)
    (send_a, send_b, field, side, fine_y, table_x, cross_fine_y, cross_x, tiles, amp) = pl.pallas_call(
        render_kernel,
        out_shape=[
            strip, strip, shape((bands, ext, width), f32), shape((ext, LANES), f32),
            shape((bands, 3 * PAD, table_width), bf16), shape((bands, width, table_width), bf16),
            shape((3 * PAD, cross_width), bf16), shape((bands * CROSS, cross_width), bf16),
            shape((2, PAD, LANES), bf16), shape(amp.shape, f32),
        ],
        in_specs=[SMEM] + [HBM] * 5,
        out_specs=[VMEM] * 10,
        scratch_shapes=[
            pltpu.VMEM(centres.shape, jnp.int32),
            pltpu.VMEM(psf_rows.shape, bf16), pltpu.VMEM(psf_cols.shape, bf16),
            pltpu.VMEM(image.shape, bf16), pltpu.SemaphoreType.DMA((5,)),
            pltpu.VMEM((comps, bands, LANES), f32), pltpu.VMEM((comps, bands, LANES), f32),
            pltpu.VMEM((comps, bands, LANES), f32),
            pltpu.VMEM((4, 3 * PAD, table_width), bf16), pltpu.VMEM((4, 3 * PAD, table_width), bf16),
            pltpu.VMEM((4, ext, table_width), bf16),
            pltpu.VMEM((3 * PAD, cross_width), bf16), pltpu.VMEM((3 * PAD, cross_width), bf16),
            pltpu.VMEM((ext, cross_width), bf16),
        ],
        compiler_params=params,
    )(scalars, *[pltpu.with_memory_space_constraint(x, pltpu.HBM) for x in (centres, amp, psf_rows, psf_cols, image)])
    cols_b = lax.ppermute(send_b, "tile", swaps("tile", 1))
    table_y, cross_y, send_a = pl.pallas_call(
        place_kernel,
        out_shape=[shape((bands, ext, table_width), bf16), shape((ext, cross_width), bf16), strip],
        in_specs=[VMEM] * 4,
        out_specs=[VMEM] * 3,
        compiler_params=params,
    )(tiles, fine_y, cross_fine_y, send_a)
    cols_a = lax.ppermute(send_a, "tile", swaps("tile", 0))
    send_a, send_b = pl.pallas_call(
        strip_kernel,
        out_shape=[shape((rows_sent, width), bf16)] * 2,
        in_specs=[SMEM] + [VMEM] * 4,
        out_specs=[VMEM] * 2,
        compiler_params=params,
    )(scalars, field, side, cols_a, cols_b)
    rows_a = lax.ppermute(send_a, "region", swaps("region", 0))
    rows_b = lax.ppermute(send_b, "region", swaps("region", 1))
    updated, residual = pl.pallas_call(
        gradient_kernel,
        out_shape=[shape(amp.shape, f32), shape(image.shape, f32)],
        in_specs=[SMEM] + [VMEM] * 11,
        out_specs=[VMEM, HBM],
        scratch_shapes=[
            pltpu.VMEM((bands, ext, width), f32), pltpu.VMEM((ext, LANES), f32),
            pltpu.VMEM((comps, bands, LANES), f32), pltpu.SemaphoreType.DMA,
        ],
        compiler_params=params,
    )(scalars, amp, field, side, cols_a, cols_b, rows_a, rows_b, table_y, table_x, cross_y, cross_x)
    return (jnp.swapaxes(updated, 0, 1)[None, None], residual)


def solution(mesh):
    in_specs = (
        P(None, "region", "tile"),
        P("region", "tile", None, None, None),
        P(None, "region", "tile", None),
        P("region", "tile"),
        P(),
        P(),
    )
    out_specs = (P("region", "tile", None, None, None), P(None, "region", "tile"))
    return jax.shard_map(
        on_device, mesh=mesh, in_specs=in_specs, out_specs=out_specs, check_vma=False
    )
```

time: 45.7 us -> 47 us (1.028)
  the two profiles are of different devices: /device:TPU:6 before, /device:TPU:56 now
where the time goes in v3:
time: 47 us; the launch traced here: 46.7 us
  starting transfers between devices  24.7 us (53%)
  Pallas kernels  10.3 us (22%)
  waiting for transfers between devices  10.2 us (22%)
  between operations  1.37 us (3%)
    ppermute x1, starting transfers between devices, on_device(): rows_b = lax.ppermute(send_b, 'region', swaps('region', 1))  16 us
    ppermute x1, waiting for transfers between devices, on_device(): rows_b = lax.ppermute(send_b, 'region', swaps('region', 1))  6.58 us
    pallas_call x1, Pallas kernels, on_device(): pl.pallas_call(render_kernel, out_shape=[strip, strip, shape((bands, ext,...  4.88 us
    ppermute x1, starting transfers between devices, on_device(): cols_b = lax.ppermute(send_b, 'tile', swaps('tile', 1))  4.22 us
    pallas_call x1, Pallas kernels, on_device(): pl.pallas_call(gradient_kernel, out_shape=[shape(amp.shape, f32), shape(i...  3.57 us
    ppermute x1, waiting for transfers between devices, on_device(): cols_a = lax.ppermute(send_a, 'tile', swaps('tile', 0))  3.35 us
    ppermute x1, starting transfers between devices, on_device(): cols_a = lax.ppermute(send_a, 'tile', swaps('tile', 0))  2.59 us
    ppermute x1, starting transfers between devices, on_device(): rows_a = lax.ppermute(send_a, 'region', swaps('region', 0))  1.92 us
  transfers between devices with their start and end apart: 4, of which 3 were waited for; matrix products, arithmetic and copies ran while one was open for 0% of the time, Pallas kernels for 3%

profile of v3, /device:TPU:56, one launch (start us, length us, event | category | flops | bytes accessed | tf_op | source)
XLA Modules:
  0.0 46.7 jit_solution(17027929256430249184)
XLA Ops:
  1.3 0.1 stack.27.scalars
  1.4 4.9 %shard_map.77 = (bf16[288,128]{1,0:T(8,128)(2,1)S(1)}, bf16[288,128]{1,0:T(8,128)(2,1)S(1)}, f32[4,288,256]{2,1,0:T(8,128)S(1)}, f32[288,128]{1,0:T(8,128)S(1)},...) custom-call(s32[7]{0:T(128)S(1)} %stack.27.scalars, ...), custom_call_target="tpu_custom_call" | custom-call | tf_op jit(solution)/shard_map/pallas_call | solution.py:294
  6.3 4.2 %collective-permute-start.1 = (bf16[288,128]{1,0:T(8,128)(2,1)S(1)}, bf16[288,128]{1,0:T(8,128)(2,1)S(1)}, u32[]{:S(2)}, u32[]{:S(2)}) collective-permute-start(bf16[288,128]{1,0:T(8,128)(2,1)S(1)} %get-tuple-element.27), channel_id=1, source_target_pairs={{1,2},{2,1},{3,4},{4,3},{5,6},{6,5},{7,8},{8,7},{9,10},{10,9},{11,... | collective-permute-start | bytes 221192 | tf_op jit(solution)/shard_map/ppermute | solution.py:317
  10.5 1.2 %shard_map.78 = (bf16[4,288,1536]{2,1,0:T(8,128)(2,1)S(1)}, bf16[288,1536]{1,0:T(8,128)(2,1)S(1)}, bf16[288,128]{1,0:T(8,128)(2,1)S(1)}) custom-call(bf16[2,16,128]{2,1,0:T(8,128)(2,1)S(1)} %get-tuple-element.22.tiles, bf16[4,48,1536]{2,1,0:T(8,128)(2,1)S(1)} %get-tuple-element.23.fine_y, bf16[48,1536]{1,0:T(8,128)(2,1)S(1)} %get-tuple-element.24.cross_fine_y, ...), custom_call_target="tpu_custom_call" | custom-call | tf_op jit(solution)/shard_map/pallas_call | solution.py:318
  11.7 2.6 %collective-permute-start = (bf16[288,128]{1,0:T(8,128)(2,1)S(1)}, bf16[288,128]{1,0:T(8,128)(2,1)S(1)}, u32[]{:S(2)}, u32[]{:S(2)}) collective-permute-start(bf16[288,128]{1,0:T(8,128)(2,1)S(1)} %get-tuple-element.26), channel_id=1, source_target_pairs={{0,1},{1,0},{2,3},{3,2},{4,5},{5,4},{6,7},{7,6},{8,9},{9,8},{10,11... | collective-permute-start | bytes 221192 | tf_op jit(solution)/shard_map/ppermute | solution.py:325
  14.3 0.3 collective-permute-done.1.got_b.cols_b
  14.6 3.3 %collective-permute-done.got_a.cols_a = bf16[288,128]{1,0:T(8,128)(2,1)S(1)} collective-permute-done((bf16[288,128]{1,0:T(8,128)(2,1)S(1)}, bf16[288,128]{1,0:T(8,128)(2,1)S(1)}, u32[]{:S(2)}, u32[]{:S(2)}) %collective-permute-start) | collective-permute-done | bytes 73760 | tf_op jit(solution)/shard_map/ppermute | solution.py:325
  18.0 0.7 %shard_map.79 = (bf16[144,256]{1,0:T(8,128)(2,1)S(1)}, bf16[144,256]{1,0:T(8,128)(2,1)S(1)}) custom-call(s32[7]{0:T(128)S(1)} %stack.27.scalars, f32[4,288,256]{2,1,0:T(8,128)S(1)} %get-tuple-element.20.field, f32[288,128]{1,0:T(8,128)S(1)} %get-tuple-element.21.side, bf16[288,128]{1,0:T(8,128)(2,1)S(1)} %collective-permute-done.got_a.cols_a, ...), custom_call_target="tpu_custom_call" | custom-call | tf_op jit(solution)/shard_map/pallas_call | solution.py:326
  18.6 1.9 %collective-permute-start.2 = (bf16[144,256]{1,0:T(8,128)(2,1)S(1)}, bf16[144,256]{1,0:T(8,128)(2,1)S(1)}, u32[]{:S(2)}, u32[]{:S(2)}) collective-permute-start(bf16[144,256]{1,0:T(8,128)(2,1)S(1)} %get-tuple-element.28), channel_id=1, source_target_pairs={{0,32},{32,0},{64,96},{96,64},{128,160},{160,128},{192,224},{224,1... | collective-permute-start | bytes 221192 | tf_op jit(solution)/shard_map/ppermute | solution.py:333
  20.6 16.0 %collective-permute-start.3 = (bf16[144,256]{1,0:T(8,128)(2,1)S(1)}, bf16[144,256]{1,0:T(8,128)(2,1)S(1)}, u32[]{:S(2)}, u32[]{:S(2)}) collective-permute-start(bf16[144,256]{1,0:T(8,128)(2,1)S(1)} %get-tuple-element.29), channel_id=1, source_target_pairs={{32,64},{64,32},{96,128},{128,96},{160,192},{192,160},{224,256},{2... | collective-permute-start | bytes 221192 | tf_op jit(solution)/shard_map/ppermute | solution.py:334
  36.6 0.0 collective-permute-done.2.rows_a
  36.6 6.6 %collective-permute-done.3.rows_b = bf16[144,256]{1,0:T(8,128)(2,1)S(1)} collective-permute-done((bf16[144,256]{1,0:T(8,128)(2,1)S(1)}, bf16[144,256]{1,0:T(8,128)(2,1)S(1)}, u32[]{:S(2)}, u32[]{:S(2)}) %collective-permute-start.3) | collective-permute-done | bytes 73760 | tf_op jit(solution)/shard_map/ppermute | solution.py:334
  43.2 3.6 %shard_map.80 = (f32[12,4,128]{2,1,0:T(4,128)}, f32[4,256,256]{2,1,0:T(8,128)}) custom-call(s32[7]{0:T(128)S(1)} %stack.27.scalars, f32[12,4,128]{2,1,0:T(4,128)S(1)} %get-tuple-element.19.amp, f32[4,288,256]{2,1,0:T(8,128)S(1)} %get-tuple-element.20.field, f32[288,128]{1,0:T(8,128)S(1)} %get-tuple-element.21.side, ...), custom_call_target="tpu_custom_call" | custom-call | tf_op jit(solution)/shard_map/pallas_call | solution.py:335
Async XLA Ops:
  6.3 8.4 %collective-permute-start.1 = (bf16[288,128]{1,0:T(8,128)(2,1)S(1)}, bf16[288,128]{1,0:T(8,128)(2,1)S(1)}, u32[]{:S(2)}, u32[]{:S(2)}) collective-permute-start(bf16[288,128]{1,0:T(8,128)(2,1)S(1)} %get-tuple-element.27), channel_id=1, source_target_pairs={{1,2},{2,1},{3,4},{4,3},{5,6},{6,5},{7,8},{8,7},{9,10},{10,9},{11,... | collective-permute-start | bytes 221192 | tf_op jit(solution)/shard_map/ppermute | solution.py:317
  11.7 6.2 %collective-permute-start = (bf16[288,128]{1,0:T(8,128)(2,1)S(1)}, bf16[288,128]{1,0:T(8,128)(2,1)S(1)}, u32[]{:S(2)}, u32[]{:S(2)}) collective-permute-start(bf16[288,128]{1,0:T(8,128)(2,1)S(1)} %get-tuple-element.26), channel_id=1, source_target_pairs={{0,1},{1,0},{2,3},{3,2},{4,5},{5,4},{6,7},{7,6},{8,9},{9,8},{10,11... | collective-permute-start | bytes 221192 | tf_op jit(solution)/shard_map/ppermute | solution.py:325
  18.6 17.9 %collective-permute-start.2 = (bf16[144,256]{1,0:T(8,128)(2,1)S(1)}, bf16[144,256]{1,0:T(8,128)(2,1)S(1)}, u32[]{:S(2)}, u32[]{:S(2)}) collective-permute-start(bf16[144,256]{1,0:T(8,128)(2,1)S(1)} %get-tuple-element.28), channel_id=1, source_target_pairs={{0,32},{32,0},{64,96},{96,64},{128,160},{160,128},{192,224},{224,1... | collective-permute-start | bytes 221192 | tf_op jit(solution)/shard_map/ppermute | solution.py:333
  20.6 22.6 %collective-permute-start.3 = (bf16[144,256]{1,0:T(8,128)(2,1)S(1)}, bf16[144,256]{1,0:T(8,128)(2,1)S(1)}, u32[]{:S(2)}, u32[]{:S(2)}) collective-permute-start(bf16[144,256]{1,0:T(8,128)(2,1)S(1)} %get-tuple-element.29), channel_id=1, source_target_pairs={{32,64},{64,32},{96,128},{128,96},{160,192},{192,160},{224,256},{2... | collective-permute-start | bytes 221192 | tf_op jit(solution)/shard_map/ppermute | solution.py:334

commit v4 on v3

--- a/solution.py
+++ b/solution.py
@@ -71,15 +71,14 @@
     return jnp.where(lane >= LANES - PAD, pltpu.roll(from_right, LANES - CROSS * b - PAD, axis=1), 0.0)
 
 
-def render_kernel(
+def edge_kernel(
     scalars, pos_hbm, amp_hbm, psf_rows_hbm, psf_cols_hbm, image_hbm,
-    send_a, send_b, field, side, fine_y, table_x, cross_fine_y, cross_x, tiles, amp,
-    pos, psf_rows, psf_cols, image, sems, tmpl_y, tmpl_x, flux,
-    fine_scaled, fine_x, scaled, cross_fine_scaled, cross_fine_x, cross_scaled,
+    send_a, send_b, fine_y, fine_scaled, table_x, cross_fine_y, cross_fine_scaled, cross_x, tiles, amp, image,
+    pos, psf_rows, psf_cols, sems, tmpl_y, tmpl_x, flux, fine_x, strips, cross_fine_x, cross_strips,
 ):
     comps, bands, taps = psf_rows.shape
-    ext, width = field.shape[1], field.shape[2]
-    height = ext - 2 * PAD
+    height, width = image.shape[1], image.shape[2]
+    even = scalars[0] == 0
     copies = [
         pltpu.make_async_copy(pos_hbm, pos, sems.at[0]),
         pltpu.make_async_copy(psf_cols_hbm, psf_cols, sems.at[1]),
@@ -130,36 +129,87 @@
                 for p in range(3):
                     value = jnp.where(cross_tile_x == tile - p, cross_fine_x[pl.ds(PAD * p, PAD), cut], value)
                 cross_x[pl.ds(b * CROSS + side_at, PAD), cut] = value
-    place(cross_scaled, cross_fine_scaled, 0, ext // PAD, cross_tile_y, 0, cross_scaled.shape[1])
-    side[...] = -lax.dot_general(cross_scaled[...], cross_x[...], NT, preferred_element_type=jnp.float32)
-
-    def one_band(b, buffers):
-        fine_scaled, fine_x, scaled = buffers
+
+    def edges(dst, src, tile, columns):
+        place(dst, src, 0, 2, tile, 0, columns)
+        place(dst, src, height // PAD, 2, tile, 2 * PAD, columns)
+
+    edges(cross_strips, cross_fine_scaled, cross_tile_y, cross_strips.shape[1])
+    wide = -lax.dot_general(cross_strips[...], cross_x[...], NT, preferred_element_type=jnp.float32)
+
+    def fill(to, top, bottom, part):
+        send_a[to, part] = jnp.where(even, bottom, top).astype(jnp.bfloat16)
+        send_b[to, part] = jnp.where(even, top, bottom).astype(jnp.bfloat16)
+
+    extra = pl.ds(bands * 2 * PAD, PAD)
+    fill(extra, wide[:PAD], wide[2 * PAD : 3 * PAD], pl.ds(0, LANES))
+    fill(extra, wide[PAD : 2 * PAD], wide[3 * PAD :], pl.ds(LANES, LANES))
+    copies[4].wait()
+    for b in range(bands):
         for k in range(comps):
             cut = pl.ds(k * LANES, LANES)
-            placed = lookup(tmpl_y[k, pl.ds(b, 1), :], index_y)
+            placed = lookup(tmpl_y[k, b : b + 1, :], index_y)
             fine_y[b, :, cut] = placed.astype(jnp.bfloat16)
-            fine_scaled[:, cut] = (placed * flux[k, pl.ds(b, 1), :]).astype(jnp.bfloat16)
-            fine_x[:, cut] = lookup(tmpl_x[k, pl.ds(b, 1), :], index_x).astype(jnp.bfloat16)
-        place(table_x.at[b], fine_x, 1, width // PAD, tile_x, 0, comps * LANES)
-        place(scaled, fine_scaled, 0, ext // PAD, tile_y, 0, comps * LANES)
-        field[b] = -lax.dot_general(scaled[...], table_x[b], NT, preferred_element_type=jnp.float32)
-
+            fine_scaled[b, :, cut] = (placed * flux[k, b : b + 1, :]).astype(jnp.bfloat16)
+            fine_x[b, :, cut] = lookup(tmpl_x[k, b : b + 1, :], index_x).astype(jnp.bfloat16)
+        place(table_x.at[b], fine_x.at[b], 1, width // PAD, tile_x, 0, comps * LANES)
+        edges(strips.at[b], fine_scaled.at[b], tile_y, comps * LANES)
+        model = -lax.dot_general(strips[b], table_x[b], NT, preferred_element_type=jnp.float32)
+        top_in = image[b, pl.ds(0, PAD), :].astype(jnp.float32)
+        bottom_in = image[b, pl.ds(height - PAD, PAD), :].astype(jnp.float32)
+        every = pl.ds(0, width)
+        fill(pl.ds(b * 2 * PAD, PAD), model[:PAD], model[2 * PAD : 3 * PAD] + bottom_in, every)
+        fill(pl.ds(b * 2 * PAD + PAD, PAD), model[PAD : 2 * PAD] + top_in, model[3 * PAD :], every)
+
+
+def pack(low, high, wide, lane):
+    to_left = to_right = wide
+    for b in range(len(low)):
+        shift = CROSS * b + PAD
+        to_left = jnp.where((lane >= shift) & (lane < shift + PAD), pltpu.roll(low[b], shift, axis=1), to_left)
+        to_right = jnp.where((lane >= shift - PAD) & (lane < shift), pltpu.roll(high[b], shift, axis=1), to_right)
+    return to_left, to_right
+
+
+def render_kernel(
+    image, tiles, fine_scaled, table_x, cross_fine_scaled, cross_x,
+    field, side, to_left, to_right, scaled, cross_scaled,
+):
+    bands, ext, width = field.shape
+    height = ext - 2 * PAD
+    lane = lax.broadcasted_iota(jnp.int32, (1, LANES), 1)
+    place(cross_scaled, cross_fine_scaled, 0, ext // PAD, tiles[1], 0, cross_scaled.shape[1])
+    side[...] = -lax.dot_general(cross_scaled[...], cross_x[...], NT, preferred_element_type=jnp.float32)
     for b in range(bands):
-        one_band(b, (fine_scaled.at[b], fine_x.at[b], scaled.at[b]))
-    copies[4].wait()
-    for b in range(bands):
-        field[b, pl.ds(PAD, height), :] += image[b].astype(jnp.float32)
-    to_left = side[...]
-    to_right = side[...]
-    for b in range(bands):
-        low = pltpu.roll(field[b, :, pl.ds(0, LANES)], CROSS * b + PAD, axis=1)
-        to_left = jnp.where((lane >= CROSS * b + PAD) & (lane < CROSS * (b + 1)), low, to_left)
-        high = pltpu.roll(field[b, :, pl.ds(width - LANES, LANES)], CROSS * b + PAD, axis=1)
-        to_right = jnp.where((lane >= CROSS * b) & (lane < CROSS * b + PAD), high, to_right)
+        place(scaled.at[b], fine_scaled.at[b], 0, ext // PAD, tiles[0], 0, scaled.shape[2])
+        model = lax.dot_general(scaled[b], table_x[b], NT, preferred_element_type=jnp.float32)
+        field[b, pl.ds(0, PAD), :] = -model[:PAD]
+        field[b, pl.ds(PAD, height), :] = image[b].astype(jnp.float32) - model[PAD : PAD + height]
+        field[b, pl.ds(PAD + height, PAD), :] = -model[PAD + height :]
+    low = [field[b, :, pl.ds(0, LANES)] for b in range(bands)]
+    high = [field[b, :, pl.ds(width - LANES, LANES)] for b in range(bands)]
+    to_left[...], to_right[...] = pack(low, high, side[...], lane)
+
+
+def column_kernel(scalars, left_in, right_in, got_b, got_a, send_a, send_b, to_left, to_right):
+    ext = left_in.shape[0]
+    lane = lax.broadcasted_iota(jnp.int32, (1, LANES), 1)
+    to_left[...] = left_in[...]
+    to_right[...] = right_in[...]
+    bands = (got_a.shape[0] - PAD) // (2 * PAD)
+    width = got_a.shape[1]
+    for got, start in zip((got_a, got_b), starts(scalars, ext - 2 * PAD)):
+        value = got[...].astype(jnp.float32)
+        low = [value[b * 2 * PAD : (b + 1) * 2 * PAD, :LANES] for b in range(bands)]
+        high = [value[b * 2 * PAD : (b + 1) * 2 * PAD, width - LANES :] for b in range(bands)]
+        extra = value[bands * 2 * PAD :]
+        wide = jnp.concatenate([extra[:, :LANES], extra[:, LANES : 2 * LANES]], axis=0)
+        left, right = pack(low, high, wide, lane)
+        to_left[pl.ds(start, 2 * PAD), :] += left
+        to_right[pl.ds(start, 2 * PAD), :] += right
     even = scalars[1] == 0
-    send_a[...] = jnp.where(even, to_right, to_left).astype(jnp.bfloat16)
-    send_b[...] = jnp.where(even, to_left, to_right).astype(jnp.bfloat16)
+    send_a[...] = jnp.where(even, to_right[...], to_left[...]).astype(jnp.bfloat16)
+    send_b[...] = jnp.where(even, to_left[...], to_right[...]).astype(jnp.bfloat16)
 
 
 def place_kernel(tiles, fine_y, cross_fine_y, ready, table_y, cross_y, send):
@@ -175,26 +225,8 @@
     place(cross_y, cross_fine_y, 0, ext // PAD, cross_tile_y, 0, cross_y.shape[1])
 
 
-def strip_kernel(scalars, field, side, got_a, got_b, send_a, send_b):
-    bands, ext, width = field.shape
-    lane = lax.broadcasted_iota(jnp.int32, (1, LANES), 1)
-    for send, start in zip((send_a, send_b), starts(scalars, ext - 2 * PAD)):
-        rows = pl.ds(start, 2 * PAD)
-        from_left, from_right = sides(scalars, got_a[rows, :], got_b[rows, :])
-        for b in range(bands):
-            to = pl.ds(b * 2 * PAD, 2 * PAD)
-            low = field[b, rows, pl.ds(0, LANES)] + low_columns(from_left, b, lane)
-            high = field[b, rows, pl.ds(width - LANES, LANES)] + high_columns(from_right, b, lane)
-            send[to, pl.ds(0, LANES)] = low.astype(jnp.bfloat16)
-            send[to, pl.ds(width - LANES, LANES)] = high.astype(jnp.bfloat16)
-        wide = side[rows, :] + jnp.where(lane % CROSS < PAD, from_left, from_right)
-        wide = wide.astype(jnp.bfloat16)
-        send[pl.ds(bands * 2 * PAD, PAD), pl.ds(0, LANES)] = wide[:PAD]
-        send[pl.ds(bands * 2 * PAD, PAD), pl.ds(LANES, LANES)] = wide[PAD:]
-
-
 def gradient_kernel(
-    scalars, amp, field, side, cols_a, cols_b, rows_a, rows_b, table_y, table_x, cross_y, cross_x,
+    scalars, amp, field, side, cols_b, cols_a, rows_b, rows_a, table_y, table_x, cross_y, cross_x,
     updated, residual, total, outer, gradient, sem,
 ):
     bands, ext, width = field.shape
@@ -291,29 +323,51 @@
     cross_width = bands * comps * CROSS
     centres = positions[:, 0, 0]
     strip = shape((ext, LANES), bf16)
-    (send_a, send_b, field, side, fine_y, table_x, cross_fine_y, cross_x, tiles, amp) = pl.pallas_call(
-        render_kernel,
+    fine = shape((bands, 3 * PAD, table_width), bf16)
+    cross_fine = shape((3 * PAD, cross_width), bf16)
+    (
+        send_a, send_b, fine_y, fine_scaled, table_x, cross_fine_y, cross_fine_scaled, cross_x, tiles, amp, image,
+    ) = pl.pallas_call(
+        edge_kernel,
         out_shape=[
-            strip, strip, shape((bands, ext, width), f32), shape((ext, LANES), f32),
-            shape((bands, 3 * PAD, table_width), bf16), shape((bands, width, table_width), bf16),
-            shape((3 * PAD, cross_width), bf16), shape((bands * CROSS, cross_width), bf16),
-            shape((2, PAD, LANES), bf16), shape(amp.shape, f32),
+            shape((rows_sent, width), bf16), shape((rows_sent, width), bf16),
+            fine, fine, shape((bands, width, table_width), bf16),
+            cross_fine, cross_fine, shape((bands * CROSS, cross_width), bf16),
+            shape((2, PAD, LANES), bf16), shape(amp.shape, f32), shape(image.shape, bf16),
         ],
         in_specs=[SMEM] + [HBM] * 5,
-        out_specs=[VMEM] * 10,
+        out_specs=[VMEM] * 11,
         scratch_shapes=[
             pltpu.VMEM(centres.shape, jnp.int32),
-            pltpu.VMEM(psf_rows.shape, bf16), pltpu.VMEM(psf_cols.shape, bf16),
-            pltpu.VMEM(image.shape, bf16), pltpu.SemaphoreType.DMA((5,)),
+            pltpu.VMEM(psf_rows.shape, bf16), pltpu.VMEM(psf_cols.shape, bf16), pltpu.SemaphoreType.DMA((5,)),
             pltpu.VMEM((comps, bands, LANES), f32), pltpu.VMEM((comps, bands, LANES), f32),
-            pltpu.VMEM((comps, bands, LANES), f32),
-            pltpu.VMEM((4, 3 * PAD, table_width), bf16), pltpu.VMEM((4, 3 * PAD, table_width), bf16),
-            pltpu.VMEM((4, ext, table_width), bf16),
-            pltpu.VMEM((3 * PAD, cross_width), bf16), pltpu.VMEM((3 * PAD, cross_width), bf16),
-            pltpu.VMEM((ext, cross_width), bf16),
+            pltpu.VMEM((comps, bands, LANES), f32), pltpu.VMEM((bands, 3 * PAD, table_width), bf16),
+            pltpu.VMEM((bands, 4 * PAD, table_width), bf16), pltpu.VMEM((3 * PAD, cross_width), bf16),
+            pltpu.VMEM((4 * PAD, cross_width), bf16),
         ],
         compiler_params=params,
     )(scalars, *[pltpu.with_memory_space_constraint(x, pltpu.HBM) for x in (centres, amp, psf_rows, psf_cols, image)])
+    rows_b = lax.ppermute(send_b, "region", swaps("region", 1))
+    rows_a = lax.ppermute(send_a, "region", swaps("region", 0))
+    field, side, to_left, to_right = pl.pallas_call(
+        render_kernel,
+        out_shape=[
+            shape((bands, ext, width), f32), shape((ext, LANES), f32),
+            shape((ext, LANES), f32), shape((ext, LANES), f32),
+        ],
+        in_specs=[VMEM] * 6,
+        out_specs=[VMEM] * 4,
+        scratch_shapes=[pltpu.VMEM((bands, ext, table_width), bf16), pltpu.VMEM((ext, cross_width), bf16)],
+        compiler_params=params,
+    )(image, tiles, fine_scaled, table_x, cross_fine_scaled, cross_x)
+    send_a, send_b = pl.pallas_call(
+        column_kernel,
+        out_shape=[strip, strip],
+        in_specs=[SMEM] + [VMEM] * 4,
+        out_specs=[VMEM] * 2,
+        scratch_shapes=[pltpu.VMEM((ext, LANES), f32), pltpu.VMEM((ext, LANES), f32)],
+        compiler_params=params,
+    )(scalars, to_left, to_right, rows_b, rows_a)
     cols_b = lax.ppermute(send_b, "tile", swaps("tile", 1))
     table_y, cross_y, send_a = pl.pallas_call(
         place_kernel,
@@ -323,15 +377,6 @@
         compiler_params=params,
     )(tiles, fine_y, cross_fine_y, send_a)
     cols_a = lax.ppermute(send_a, "tile", swaps("tile", 0))
-    send_a, send_b = pl.pallas_call(
-        strip_kernel,
-        out_shape=[shape((rows_sent, width), bf16)] * 2,
-        in_specs=[SMEM] + [VMEM] * 4,
-        out_specs=[VMEM] * 2,
-        compiler_params=params,
-    )(scalars, field, side, cols_a, cols_b)
-    rows_a = lax.ppermute(send_a, "region", swaps("region", 0))
-    rows_b = lax.ppermute(send_b, "region", swaps("region", 1))
     updated, residual = pl.pallas_call(
         gradient_kernel,
         out_shape=[shape(amp.shape, f32), shape(image.shape, f32)],
@@ -342,7 +387,7 @@
             pltpu.VMEM((comps, bands, LANES), f32), pltpu.SemaphoreType.DMA,
         ],
         compiler_params=params,
-    )(scalars, amp, field, side, cols_a, cols_b, rows_a, rows_b, table_y, table_x, cross_y, cross_x)
+    )(scalars, amp, field, side, cols_b, cols_a, rows_b, rows_a, table_y, table_x, cross_y, cross_x)
     return (jnp.swapaxes(updated, 0, 1)[None, None], residual)
 
 

time: 47 us -> 43.1 us (0.917)
  the two profiles are of different devices: /device:TPU:56 before, /device:TPU:88 now
where the time goes in v4:
time: 43.1 us; the launch traced here: 42.9 us
  starting transfers between devices  25.4 us (59%)
  Pallas kernels  11.5 us (27%)
  waiting for transfers between devices  4.57 us (11%)
  between operations  1.37 us (3%)
    ppermute x1, starting transfers between devices, on_device(): rows_b = lax.ppermute(send_b, 'region', swaps('region', 1))  13.5 us
    ppermute x1, starting transfers between devices, on_device(): cols_b = lax.ppermute(send_b, 'tile', swaps('tile', 1))  7.52 us
    ppermute x1, waiting for transfers between devices, on_device(): cols_a = lax.ppermute(send_a, 'tile', swaps('tile', 0))  4.31 us
    pallas_call x1, Pallas kernels, on_device(): pl.pallas_call(edge_kernel, out_shape=[shape((rows_sent, width), bf16), s...  3.87 us
    pallas_call x1, Pallas kernels, on_device(): pl.pallas_call(gradient_kernel, out_shape=[shape(amp.shape, f32), shape(i...  3.57 us
    ppermute x1, starting transfers between devices, on_device(): rows_a = lax.ppermute(send_a, 'region', swaps('region', 0))  2.4 us
    pallas_call x1, Pallas kernels, on_device(): pl.pallas_call(render_kernel, out_shape=[shape((bands, ext, width), f32),...  2.13 us
    ppermute x1, starting transfers between devices, on_device(): cols_a = lax.ppermute(send_a, 'tile', swaps('tile', 0))  1.92 us
  transfers between devices with their start and end apart: 4, of which 2 were waited for; matrix products, arithmetic and copies ran while one was open for 0% of the time, Pallas kernels for 8%

profile of v4, /device:TPU:88, one launch (start us, length us, event | category | flops | bytes accessed | tf_op | source)
XLA Modules:
  0.0 42.9 jit_solution(14084611181473047428)
XLA Ops:
  1.3 0.1 stack.27.scalars
  1.4 3.9 %shard_map.77 = (bf16[144,256]{1,0:T(8,128)(2,1)S(1)}, bf16[144,256]{1,0:T(8,128)(2,1)S(1)}, bf16[4,48,1536]{2,1,0:T(8,128)(2,1)S(1)}, bf16[4,48,1536]{2,1,0:T(8...) custom-call(s32[7]{0:T(128)S(1)} %stack.27.scalars, ...), custom_call_target="tpu_custom_call" | custom-call | tf_op jit(solution)/shard_map/pallas_call | solution.py:330
  5.3 13.5 %collective-permute-start = (bf16[144,256]{1,0:T(8,128)(2,1)S(1)}, bf16[144,256]{1,0:T(8,128)(2,1)S(1)}, u32[]{:S(2)}, u32[]{:S(2)}) collective-permute-start(bf16[144,256]{1,0:T(8,128)(2,1)S(1)} %get-tuple-element.35), channel_id=1, source_target_pairs={{32,64},{64,32},{96,128},{128,96},{160,192},{192,160},{224,256},{2... | collective-permute-start | bytes 221192 | tf_op jit(solution)/shard_map/ppermute | solution.py:350
  18.8 2.4 %collective-permute-start.1 = (bf16[144,256]{1,0:T(8,128)(2,1)S(1)}, bf16[144,256]{1,0:T(8,128)(2,1)S(1)}, u32[]{:S(2)}, u32[]{:S(2)}) collective-permute-start(bf16[144,256]{1,0:T(8,128)(2,1)S(1)} %get-tuple-element.36), channel_id=1, source_target_pairs={{0,32},{32,0},{64,96},{96,64},{128,160},{160,128},{192,224},{224,1... | collective-permute-start | bytes 221192 | tf_op jit(solution)/shard_map/ppermute | solution.py:351
  21.2 2.1 %shard_map.78 = (f32[4,288,256]{2,1,0:T(8,128)S(1)}, f32[288,128]{1,0:T(8,128)S(1)}, f32[288,128]{1,0:T(8,128)S(1)}, f32[288,128]{1,0:T(8,128)S(1)}) custom-call(bf16[4,256,256]{2,1,0:T(8,128)(2,1)S(1)} %get-tuple-element.25.image, bf16[2,16,128]{2,1,0:T(8,128)(2,1)S(1)} %get-tuple-element.26.tiles, bf16[4,48,1536]{2,1,0:T(8,128)(2,1)S(1)} %get-tuple-element.27.fine_scaled, ...), custom_call_target="tpu_custom_call" | custom-call | tf_op jit(solution)/shard_map/pallas_call | solution.py:352
  23.4 0.3 collective-permute-done.got_b.rows_b
  23.6 0.0 collective-permute-done.1.got_a.rows_a
  23.6 0.7 %shard_map.79 = (bf16[288,128]{1,0:T(8,128)(2,1)S(1)}, bf16[288,128]{1,0:T(8,128)(2,1)S(1)}) custom-call(s32[7]{0:T(128)S(1)} %stack.27.scalars, f32[288,128]{1,0:T(8,128)S(1)} %get-tuple-element.33.left_in, f32[288,128]{1,0:T(8,128)S(1)} %get-tuple-element.34.right_in, bf16[144,256]{1,0:T(8,128)(2,1)S(1)} %collective-permute-done.got_b.rows_b, ...), custom_call_target="tpu_custom_call" | custom-call | tf_op jit(solution)/shard_map/pallas_call | solution.py:363
  24.3 7.5 %collective-permute-start.2 = (bf16[288,128]{1,0:T(8,128)(2,1)S(1)}, bf16[288,128]{1,0:T(8,128)(2,1)S(1)}, u32[]{:S(2)}, u32[]{:S(2)}) collective-permute-start(bf16[288,128]{1,0:T(8,128)(2,1)S(1)} %get-tuple-element.37), channel_id=1, source_target_pairs={{1,2},{2,1},{3,4},{4,3},{5,6},{6,5},{7,8},{8,7},{9,10},{10,9},{11,... | collective-permute-start | bytes 221192 | tf_op jit(solution)/shard_map/ppermute | solution.py:371
  31.8 1.2 %shard_map.80 = (bf16[4,288,1536]{2,1,0:T(8,128)(2,1)S(1)}, bf16[288,1536]{1,0:T(8,128)(2,1)S(1)}, bf16[288,128]{1,0:T(8,128)(2,1)S(1)}) custom-call(bf16[2,16,128]{2,1,0:T(8,128)(2,1)S(1)} %get-tuple-element.26.tiles, bf16[4,48,1536]{2,1,0:T(8,128)(2,1)S(1)} %get-tuple-element.38.fine_y, bf16[48,1536]{1,0:T(8,128)(2,1)S(1)} %get-tuple-element.39.cross_fine_y, ...), custom_call_target="tpu_custom_call" | custom-call | tf_op jit(solution)/shard_map/pallas_call | solution.py:372
  33.1 1.9 %collective-permute-start.3 = (bf16[288,128]{1,0:T(8,128)(2,1)S(1)}, bf16[288,128]{1,0:T(8,128)(2,1)S(1)}, u32[]{:S(2)}, u32[]{:S(2)}) collective-permute-start(bf16[288,128]{1,0:T(8,128)(2,1)S(1)} %get-tuple-element.41), channel_id=1, source_target_pairs={{0,1},{1,0},{2,3},{3,2},{4,5},{5,4},{6,7},{7,6},{8,9},{9,8},{10,11... | collective-permute-start | bytes 221192 | tf_op jit(solution)/shard_map/ppermute | solution.py:379
  35.0 0.0 collective-permute-done.2.cols_b
  35.0 4.3 %collective-permute-done.3.cols_a = bf16[288,128]{1,0:T(8,128)(2,1)S(1)} collective-permute-done((bf16[288,128]{1,0:T(8,128)(2,1)S(1)}, bf16[288,128]{1,0:T(8,128)(2,1)S(1)}, u32[]{:S(2)}, u32[]{:S(2)}) %collective-permute-start.3) | collective-permute-done | bytes 73760 | tf_op jit(solution)/shard_map/ppermute | solution.py:379
  39.3 3.6 %shard_map.81 = (f32[12,4,128]{2,1,0:T(4,128)}, f32[4,256,256]{2,1,0:T(8,128)}) custom-call(s32[7]{0:T(128)S(1)} %stack.27.scalars, f32[12,4,128]{2,1,0:T(4,128)S(1)} %get-tuple-element.24.amp, f32[4,288,256]{2,1,0:T(8,128)S(1)} %get-tuple-element.31.field, f32[288,128]{1,0:T(8,128)S(1)} %get-tuple-element.32.side, ...), custom_call_target="tpu_custom_call" | custom-call | tf_op jit(solution)/shard_map/pallas_call | solution.py:380
Async XLA Ops:
  5.3 18.4 %collective-permute-start = (bf16[144,256]{1,0:T(8,128)(2,1)S(1)}, bf16[144,256]{1,0:T(8,128)(2,1)S(1)}, u32[]{:S(2)}, u32[]{:S(2)}) collective-permute-start(bf16[144,256]{1,0:T(8,128)(2,1)S(1)} %get-tuple-element.35), channel_id=1, source_target_pairs={{32,64},{64,32},{96,128},{128,96},{160,192},{192,160},{224,256},{2... | collective-permute-start | bytes 221192 | tf_op jit(solution)/shard_map/ppermute | solution.py:350
  18.8 4.8 %collective-permute-start.1 = (bf16[144,256]{1,0:T(8,128)(2,1)S(1)}, bf16[144,256]{1,0:T(8,128)(2,1)S(1)}, u32[]{:S(2)}, u32[]{:S(2)}) collective-permute-start(bf16[144,256]{1,0:T(8,128)(2,1)S(1)} %get-tuple-element.36), channel_id=1, source_target_pairs={{0,32},{32,0},{64,96},{96,64},{128,160},{160,128},{192,224},{224,1... | collective-permute-start | bytes 221192 | tf_op jit(solution)/shard_map/ppermute | solution.py:351
  24.3 10.7 %collective-permute-start.2 = (bf16[288,128]{1,0:T(8,128)(2,1)S(1)}, bf16[288,128]{1,0:T(8,128)(2,1)S(1)}, u32[]{:S(2)}, u32[]{:S(2)}) collective-permute-start(bf16[288,128]{1,0:T(8,128)(2,1)S(1)} %get-tuple-element.37), channel_id=1, source_target_pairs={{1,2},{2,1},{3,4},{4,3},{5,6},{6,5},{7,8},{8,7},{9,10},{10,9},{11,... | collective-permute-start | bytes 221192 | tf_op jit(solution)/shard_map/ppermute | solution.py:371
  33.1 6.2 %collective-permute-start.3 = (bf16[288,128]{1,0:T(8,128)(2,1)S(1)}, bf16[288,128]{1,0:T(8,128)(2,1)S(1)}, u32[]{:S(2)}, u32[]{:S(2)}) collective-permute-start(bf16[288,128]{1,0:T(8,128)(2,1)S(1)} %get-tuple-element.41), channel_id=1, source_target_pairs={{0,1},{1,0},{2,3},{3,2},{4,5},{5,4},{6,7},{7,6},{8,9},{9,8},{10,11... | collective-permute-start | bytes 221192 | tf_op jit(solution)/shard_map/ppermute | solution.py:379

commit v5 on v4

--- a/solution.py
+++ b/solution.py
@@ -212,7 +212,7 @@
     send_b[...] = jnp.where(even, to_left[...], to_right[...]).astype(jnp.bfloat16)
 
 
-def place_kernel(tiles, fine_y, cross_fine_y, ready, table_y, cross_y, send):
+def place_kernel(tiles, fine_y, cross_fine_y, ready, table_y, cross_y):
     bands, ext, columns = table_y.shape
     tile_y, cross_tile_y = tiles[0], tiles[1]
 
@@ -220,7 +220,6 @@
         place(table_y.at[b], fine_y.at[b], 0, ext // PAD, tile_y, 0, columns)
         return carry
 
-    send[...] = ready[...]
     lax.fori_loop(0, bands, one_band, 0)
     place(cross_y, cross_fine_y, 0, ext // PAD, cross_tile_y, 0, cross_y.shape[1])
 
@@ -254,25 +253,16 @@
     inside = inside & (lane % CROSS >= low_col) & (lane % CROSS < high_col)
     beyond = jnp.where(inside, outer[...], 0.0).astype(jnp.bfloat16)
 
-    @pl.when(low_row > 0)
-    def _():
-        total[:, pl.ds(0, PAD), :] = jnp.zeros((bands, PAD, width), jnp.float32)
-
-    @pl.when(high_row < ext)
-    def _():
-        total[:, pl.ds(ext - PAD, PAD), :] = jnp.zeros((bands, PAD, width), jnp.float32)
-
-    def one_band(b, carry):
+    total[:, pl.ds(0, PAD), :] = jnp.where(low_row > 0, 0.0, total[:, pl.ds(0, PAD), :])
+    total[:, pl.ds(ext - PAD, PAD), :] = jnp.where(high_row < ext, 0.0, total[:, pl.ds(ext - PAD, PAD), :])
+    for b in range(bands):
         rounded = total[b].astype(jnp.bfloat16)
         for k in range(0, comps, 2):
             cut = pl.ds(k * LANES, 2 * LANES)
             inner = lax.dot_general(rounded, table_x[b, :, cut], NN, preferred_element_type=jnp.float32)
             summed = jnp.sum(inner * table_y[b, :, cut].astype(jnp.float32), axis=0, keepdims=True)
-            gradient[k, pl.ds(b, 1), :] = summed[:, :LANES]
-            gradient[k + 1, pl.ds(b, 1), :] = summed[:, LANES:]
-        return carry
-
-    lax.fori_loop(0, bands, one_band, 0)
+            gradient[k, b : b + 1, :] = summed[:, :LANES]
+            gradient[k + 1, b : b + 1, :] = summed[:, LANES:]
 
     inner = lax.dot_general(beyond, cross_x[...], NN, preferred_element_type=jnp.float32)
     summed = jnp.sum(inner * cross_y[...].astype(jnp.float32), axis=0, keepdims=True)
@@ -369,14 +359,14 @@
         compiler_params=params,
     )(scalars, to_left, to_right, rows_b, rows_a)
     cols_b = lax.ppermute(send_b, "tile", swaps("tile", 1))
-    table_y, cross_y, send_a = pl.pallas_call(
+    cols_a = lax.ppermute(send_a, "tile", swaps("tile", 0))
+    table_y, cross_y = pl.pallas_call(
         place_kernel,
-        out_shape=[shape((bands, ext, table_width), bf16), shape((ext, cross_width), bf16), strip],
+        out_shape=[shape((bands, ext, table_width), bf16), shape((ext, cross_width), bf16)],
         in_specs=[VMEM] * 4,
-        out_specs=[VMEM] * 3,
+        out_specs=[VMEM] * 2,
         compiler_params=params,
     )(tiles, fine_y, cross_fine_y, send_a)
-    cols_a = lax.ppermute(send_a, "tile", swaps("tile", 0))
     updated, residual = pl.pallas_call(
         gradient_kernel,
         out_shape=[shape(amp.shape, f32), shape(image.shape, f32)],

time: 43.1 us -> 41.1 us (0.954)
  waiting for transfers between devices: 4.57 us -> 3.34 us
  Pallas kernels: 11.5 us -> 10.7 us
    ppermute x1, waiting for transfers between devices: 4.31 us -> 3.08 us  [on_device(): cols_a = lax.ppermute(send_a, 'tile', swaps('tile', 0))]
    pallas_call x1, Pallas kernels: 3.57 us -> 2.82 us  [on_device(): pl.pallas_call(gradient_kernel, out_shape=[shape(amp.shape, f32), shape(i...]
where the time goes in v5:
time: 41.1 us; the launch traced here: 40.9 us
  starting transfers between devices  25.4 us (62%)
  Pallas kernels  10.7 us (26%)
  waiting for transfers between devices  3.34 us (8%)
  between operations  1.37 us (3%)
    ppermute x1, starting transfers between devices, on_device(): rows_b = lax.ppermute(send_b, 'region', swaps('region', 1))  13.6 us
    ppermute x1, starting transfers between devices, on_device(): cols_b = lax.ppermute(send_b, 'tile', swaps('tile', 1))  7.52 us
    pallas_call x1, Pallas kernels, on_device(): pl.pallas_call(edge_kernel, out_shape=[shape((rows_sent, width), bf16), s...  3.86 us
    ppermute x1, waiting for transfers between devices, on_device(): cols_a = lax.ppermute(send_a, 'tile', swaps('tile', 0))  3.08 us
    pallas_call x1, Pallas kernels, on_device(): pl.pallas_call(gradient_kernel, out_shape=[shape(amp.shape, f32), shape(i...  2.82 us
    ppermute x1, starting transfers between devices, on_device(): rows_a = lax.ppermute(send_a, 'region', swaps('region', 0))  2.4 us
    pallas_call x1, Pallas kernels, on_device(): pl.pallas_call(render_kernel, out_shape=[shape((bands, ext, width), f32),...  2.13 us
    ppermute x1, starting transfers between devices, on_device(): cols_a = lax.ppermute(send_a, 'tile', swaps('tile', 0))  1.92 us
  transfers between devices with their start and end apart: 4, of which 2 were waited for; matrix products, arithmetic and copies ran while one was open for 0% of the time, Pallas kernels for 8%

profile of v5, /device:TPU:88, one launch (start us, length us, event | category | flops | bytes accessed | tf_op | source)
XLA Modules:
  0.0 40.9 jit_solution(8679791871189335870)
XLA Ops:
  1.3 0.1 stack.27.scalars
  1.4 3.9 %shard_map.77 = (bf16[144,256]{1,0:T(8,128)(2,1)S(1)}, bf16[144,256]{1,0:T(8,128)(2,1)S(1)}, bf16[4,48,1536]{2,1,0:T(8,128)(2,1)S(1)}, bf16[4,48,1536]{2,1,0:T(8...) custom-call(s32[7]{0:T(128)S(1)} %stack.27.scalars, ...), custom_call_target="tpu_custom_call" | custom-call | tf_op jit(solution)/shard_map/pallas_call | solution.py:320
  5.3 13.6 %collective-permute-start = (bf16[144,256]{1,0:T(8,128)(2,1)S(1)}, bf16[144,256]{1,0:T(8,128)(2,1)S(1)}, u32[]{:S(2)}, u32[]{:S(2)}) collective-permute-start(bf16[144,256]{1,0:T(8,128)(2,1)S(1)} %get-tuple-element.34), channel_id=1, source_target_pairs={{32,64},{64,32},{96,128},{128,96},{160,192},{192,160},{224,256},{2... | collective-permute-start | bytes 221192 | tf_op jit(solution)/shard_map/ppermute | solution.py:340
  18.8 2.4 %collective-permute-start.1 = (bf16[144,256]{1,0:T(8,128)(2,1)S(1)}, bf16[144,256]{1,0:T(8,128)(2,1)S(1)}, u32[]{:S(2)}, u32[]{:S(2)}) collective-permute-start(bf16[144,256]{1,0:T(8,128)(2,1)S(1)} %get-tuple-element.35), channel_id=1, source_target_pairs={{0,32},{32,0},{64,96},{96,64},{128,160},{160,128},{192,224},{224,1... | collective-permute-start | bytes 221192 | tf_op jit(solution)/shard_map/ppermute | solution.py:341
  21.2 2.1 %shard_map.78 = (f32[4,288,256]{2,1,0:T(8,128)S(1)}, f32[288,128]{1,0:T(8,128)S(1)}, f32[288,128]{1,0:T(8,128)S(1)}, f32[288,128]{1,0:T(8,128)S(1)}) custom-call(bf16[4,256,256]{2,1,0:T(8,128)(2,1)S(1)} %get-tuple-element.24.image, bf16[2,16,128]{2,1,0:T(8,128)(2,1)S(1)} %get-tuple-element.25.tiles, bf16[4,48,1536]{2,1,0:T(8,128)(2,1)S(1)} %get-tuple-element.26.fine_scaled, ...), custom_call_target="tpu_custom_call" | custom-call | tf_op jit(solution)/shard_map/pallas_call | solution.py:342
  23.4 0.3 collective-permute-done.got_b.rows_b
  23.6 0.0 collective-permute-done.1.got_a.rows_a
  23.6 0.7 %shard_map.79 = (bf16[288,128]{1,0:T(8,128)(2,1)S(1)}, bf16[288,128]{1,0:T(8,128)(2,1)S(1)}) custom-call(s32[7]{0:T(128)S(1)} %stack.27.scalars, f32[288,128]{1,0:T(8,128)S(1)} %get-tuple-element.32.left_in, f32[288,128]{1,0:T(8,128)S(1)} %get-tuple-element.33.right_in, bf16[144,256]{1,0:T(8,128)(2,1)S(1)} %collective-permute-done.got_b.rows_b, ...), custom_call_target="tpu_custom_call" | custom-call | tf_op jit(solution)/shard_map/pallas_call | solution.py:353
  24.3 7.5 %collective-permute-start.2 = (bf16[288,128]{1,0:T(8,128)(2,1)S(1)}, bf16[288,128]{1,0:T(8,128)(2,1)S(1)}, u32[]{:S(2)}, u32[]{:S(2)}) collective-permute-start(bf16[288,128]{1,0:T(8,128)(2,1)S(1)} %get-tuple-element.36), channel_id=1, source_target_pairs={{1,2},{2,1},{3,4},{4,3},{5,6},{6,5},{7,8},{8,7},{9,10},{10,9},{11,... | collective-permute-start | bytes 221192 | tf_op jit(solution)/shard_map/ppermute | solution.py:361
  31.8 1.9 %collective-permute-start.3 = (bf16[288,128]{1,0:T(8,128)(2,1)S(1)}, bf16[288,128]{1,0:T(8,128)(2,1)S(1)}, u32[]{:S(2)}, u32[]{:S(2)}) collective-permute-start(bf16[288,128]{1,0:T(8,128)(2,1)S(1)} %get-tuple-element.37.ready), channel_id=1, source_target_pairs={{0,1},{1,0},{2,3},{3,2},{4,5},{5,4},{6,7},{7,6},{8,9},{9,8},{10,11... | collective-permute-start | bytes 221192 | tf_op jit(solution)/shard_map/ppermute | solution.py:362
  33.7 1.2 %shard_map.80 = (bf16[4,288,1536]{2,1,0:T(8,128)(2,1)S(1)}, bf16[288,1536]{1,0:T(8,128)(2,1)S(1)}) custom-call(bf16[2,16,128]{2,1,0:T(8,128)(2,1)S(1)} %get-tuple-element.25.tiles, bf16[4,48,1536]{2,1,0:T(8,128)(2,1)S(1)} %get-tuple-element.38.fine_y, bf16[48,1536]{1,0:T(8,128)(2,1)S(1)} %get-tuple-element.39.cross_fine_y, ...), custom_call_target="tpu_custom_call" | custom-call | tf_op jit(solution)/shard_map/pallas_call | solution.py:363
  35.0 0.0 collective-permute-done.2.cols_b
  35.0 3.1 %collective-permute-done.3.cols_a = bf16[288,128]{1,0:T(8,128)(2,1)S(1)} collective-permute-done((bf16[288,128]{1,0:T(8,128)(2,1)S(1)}, bf16[288,128]{1,0:T(8,128)(2,1)S(1)}, u32[]{:S(2)}, u32[]{:S(2)}) %collective-permute-start.3) | collective-permute-done | bytes 73760 | tf_op jit(solution)/shard_map/ppermute | solution.py:362
  38.1 2.8 %shard_map.81 = (f32[12,4,128]{2,1,0:T(4,128)}, f32[4,256,256]{2,1,0:T(8,128)}) custom-call(s32[7]{0:T(128)S(1)} %stack.27.scalars, f32[12,4,128]{2,1,0:T(4,128)S(1)} %get-tuple-element.23.amp, f32[4,288,256]{2,1,0:T(8,128)S(1)} %get-tuple-element.30.field, f32[288,128]{1,0:T(8,128)S(1)} %get-tuple-element.31.side, ...), custom_call_target="tpu_custom_call" | custom-call | tf_op jit(solution)/shard_map/pallas_call | solution.py:370
Async XLA Ops:
  5.3 18.4 %collective-permute-start = (bf16[144,256]{1,0:T(8,128)(2,1)S(1)}, bf16[144,256]{1,0:T(8,128)(2,1)S(1)}, u32[]{:S(2)}, u32[]{:S(2)}) collective-permute-start(bf16[144,256]{1,0:T(8,128)(2,1)S(1)} %get-tuple-element.34), channel_id=1, source_target_pairs={{32,64},{64,32},{96,128},{128,96},{160,192},{192,160},{224,256},{2... | collective-permute-start | bytes 221192 | tf_op jit(solution)/shard_map/ppermute | solution.py:340
  18.8 4.8 %collective-permute-start.1 = (bf16[144,256]{1,0:T(8,128)(2,1)S(1)}, bf16[144,256]{1,0:T(8,128)(2,1)S(1)}, u32[]{:S(2)}, u32[]{:S(2)}) collective-permute-start(bf16[144,256]{1,0:T(8,128)(2,1)S(1)} %get-tuple-element.35), channel_id=1, source_target_pairs={{0,32},{32,0},{64,96},{96,64},{128,160},{160,128},{192,224},{224,1... | collective-permute-start | bytes 221192 | tf_op jit(solution)/shard_map/ppermute | solution.py:341
  24.3 10.7 %collective-permute-start.2 = (bf16[288,128]{1,0:T(8,128)(2,1)S(1)}, bf16[288,128]{1,0:T(8,128)(2,1)S(1)}, u32[]{:S(2)}, u32[]{:S(2)}) collective-permute-start(bf16[288,128]{1,0:T(8,128)(2,1)S(1)} %get-tuple-element.36), channel_id=1, source_target_pairs={{1,2},{2,1},{3,4},{4,3},{5,6},{6,5},{7,8},{8,7},{9,10},{10,9},{11,... | collective-permute-start | bytes 221192 | tf_op jit(solution)/shard_map/ppermute | solution.py:361
  31.8 6.2 %collective-permute-start.3 = (bf16[288,128]{1,0:T(8,128)(2,1)S(1)}, bf16[288,128]{1,0:T(8,128)(2,1)S(1)}, u32[]{:S(2)}, u32[]{:S(2)}) collective-permute-start(bf16[288,128]{1,0:T(8,128)(2,1)S(1)} %get-tuple-element.37.ready), channel_id=1, source_target_pairs={{0,1},{1,0},{2,3},{3,2},{4,5},{5,4},{6,7},{7,6},{8,9},{9,8},{10,11... | collective-permute-start | bytes 221192 | tf_op jit(solution)/shard_map/ppermute | solution.py:362

commit v6 on v5

--- a/solution.py
+++ b/solution.py
@@ -144,7 +144,6 @@
     extra = pl.ds(bands * 2 * PAD, PAD)
     fill(extra, wide[:PAD], wide[2 * PAD : 3 * PAD], pl.ds(0, LANES))
     fill(extra, wide[PAD : 2 * PAD], wide[3 * PAD :], pl.ds(LANES, LANES))
-    copies[4].wait()
     for b in range(bands):
         for k in range(comps):
             cut = pl.ds(k * LANES, LANES)
@@ -155,6 +154,8 @@
         place(table_x.at[b], fine_x.at[b], 1, width // PAD, tile_x, 0, comps * LANES)
         edges(strips.at[b], fine_scaled.at[b], tile_y, comps * LANES)
         model = -lax.dot_general(strips[b], table_x[b], NT, preferred_element_type=jnp.float32)
+        if b == 0:
+            copies[4].wait()
         top_in = image[b, pl.ds(0, PAD), :].astype(jnp.float32)
         bottom_in = image[b, pl.ds(height - PAD, PAD), :].astype(jnp.float32)
         every = pl.ds(0, width)

time: 41.1 us -> 41.1 us (level)
  no operation moved by 1% of the time
where the time goes in v6:
time: 41.1 us; the launch traced here: 40.9 us
  starting transfers between devices  25.4 us (62%)
  Pallas kernels  10.7 us (26%)
  waiting for transfers between devices  3.34 us (8%)
  between operations  1.37 us (3%)
    ppermute x1, starting transfers between devices, on_device(): rows_b = lax.ppermute(send_b, 'region', swaps('region', 1))  13.5 us
    ppermute x1, starting transfers between devices, on_device(): cols_b = lax.ppermute(send_b, 'tile', swaps('tile', 1))  7.52 us
    pallas_call x1, Pallas kernels, on_device(): pl.pallas_call(edge_kernel, out_shape=[shape((rows_sent, width), bf16), s...  3.84 us
    ppermute x1, waiting for transfers between devices, on_device(): cols_a = lax.ppermute(send_a, 'tile', swaps('tile', 0))  3.08 us
    pallas_call x1, Pallas kernels, on_device(): pl.pallas_call(gradient_kernel, out_shape=[shape(amp.shape, f32), shape(i...  2.82 us
    ppermute x1, starting transfers between devices, on_device(): rows_a = lax.ppermute(send_a, 'region', swaps('region', 0))  2.4 us
    pallas_call x1, Pallas kernels, on_device(): pl.pallas_call(render_kernel, out_shape=[shape((bands, ext, width), f32),...  2.13 us
    ppermute x1, starting transfers between devices, on_device(): cols_a = lax.ppermute(send_a, 'tile', swaps('tile', 0))  1.92 us
  transfers between devices with their start and end apart: 4, of which 2 were waited for; matrix products, arithmetic and copies ran while one was open for 0% of the time, Pallas kernels for 8%

profile of v6, /device:TPU:88, one launch (start us, length us, event | category | flops | bytes accessed | tf_op | source)
XLA Modules:
  0.0 40.9 jit_solution(11167717949376321649)
XLA Ops:
  1.3 0.1 stack.27.scalars
  1.4 3.8 %shard_map.77 = (bf16[144,256]{1,0:T(8,128)(2,1)S(1)}, bf16[144,256]{1,0:T(8,128)(2,1)S(1)}, bf16[4,48,1536]{2,1,0:T(8,128)(2,1)S(1)}, bf16[4,48,1536]{2,1,0:T(8...) custom-call(s32[7]{0:T(128)S(1)} %stack.27.scalars, ...), custom_call_target="tpu_custom_call" | custom-call | tf_op jit(solution)/shard_map/pallas_call | solution.py:321
  5.2 13.5 %collective-permute-start = (bf16[144,256]{1,0:T(8,128)(2,1)S(1)}, bf16[144,256]{1,0:T(8,128)(2,1)S(1)}, u32[]{:S(2)}, u32[]{:S(2)}) collective-permute-start(bf16[144,256]{1,0:T(8,128)(2,1)S(1)} %get-tuple-element.34), channel_id=1, source_target_pairs={{32,64},{64,32},{96,128},{128,96},{160,192},{192,160},{224,256},{2... | collective-permute-start | bytes 221192 | tf_op jit(solution)/shard_map/ppermute | solution.py:341
  18.8 2.4 %collective-permute-start.1 = (bf16[144,256]{1,0:T(8,128)(2,1)S(1)}, bf16[144,256]{1,0:T(8,128)(2,1)S(1)}, u32[]{:S(2)}, u32[]{:S(2)}) collective-permute-start(bf16[144,256]{1,0:T(8,128)(2,1)S(1)} %get-tuple-element.35), channel_id=1, source_target_pairs={{0,32},{32,0},{64,96},{96,64},{128,160},{160,128},{192,224},{224,1... | collective-permute-start | bytes 221192 | tf_op jit(solution)/shard_map/ppermute | solution.py:342
  21.2 2.1 %shard_map.78 = (f32[4,288,256]{2,1,0:T(8,128)S(1)}, f32[288,128]{1,0:T(8,128)S(1)}, f32[288,128]{1,0:T(8,128)S(1)}, f32[288,128]{1,0:T(8,128)S(1)}) custom-call(bf16[4,256,256]{2,1,0:T(8,128)(2,1)S(1)} %get-tuple-element.24.image, bf16[2,16,128]{2,1,0:T(8,128)(2,1)S(1)} %get-tuple-element.25.tiles, bf16[4,48,1536]{2,1,0:T(8,128)(2,1)S(1)} %get-tuple-element.26.fine_scaled, ...), custom_call_target="tpu_custom_call" | custom-call | tf_op jit(solution)/shard_map/pallas_call | solution.py:343
  23.3 0.3 collective-permute-done.got_b.rows_b
  23.6 0.0 collective-permute-done.1.got_a.rows_a
  23.6 0.7 %shard_map.79 = (bf16[288,128]{1,0:T(8,128)(2,1)S(1)}, bf16[288,128]{1,0:T(8,128)(2,1)S(1)}) custom-call(s32[7]{0:T(128)S(1)} %stack.27.scalars, f32[288,128]{1,0:T(8,128)S(1)} %get-tuple-element.32.left_in, f32[288,128]{1,0:T(8,128)S(1)} %get-tuple-element.33.right_in, bf16[144,256]{1,0:T(8,128)(2,1)S(1)} %collective-permute-done.got_b.rows_b, ...), custom_call_target="tpu_custom_call" | custom-call | tf_op jit(solution)/shard_map/pallas_call | solution.py:354
  24.3 7.5 %collective-permute-start.2 = (bf16[288,128]{1,0:T(8,128)(2,1)S(1)}, bf16[288,128]{1,0:T(8,128)(2,1)S(1)}, u32[]{:S(2)}, u32[]{:S(2)}) collective-permute-start(bf16[288,128]{1,0:T(8,128)(2,1)S(1)} %get-tuple-element.36), channel_id=1, source_target_pairs={{1,2},{2,1},{3,4},{4,3},{5,6},{6,5},{7,8},{8,7},{9,10},{10,9},{11,... | collective-permute-start | bytes 221192 | tf_op jit(solution)/shard_map/ppermute | solution.py:362
  31.8 1.9 %collective-permute-start.3 = (bf16[288,128]{1,0:T(8,128)(2,1)S(1)}, bf16[288,128]{1,0:T(8,128)(2,1)S(1)}, u32[]{:S(2)}, u32[]{:S(2)}) collective-permute-start(bf16[288,128]{1,0:T(8,128)(2,1)S(1)} %get-tuple-element.37.ready), channel_id=1, source_target_pairs={{0,1},{1,0},{2,3},{3,2},{4,5},{5,4},{6,7},{7,6},{8,9},{9,8},{10,11... | collective-permute-start | bytes 221192 | tf_op jit(solution)/shard_map/ppermute | solution.py:363
  33.7 1.2 %shard_map.80 = (bf16[4,288,1536]{2,1,0:T(8,128)(2,1)S(1)}, bf16[288,1536]{1,0:T(8,128)(2,1)S(1)}) custom-call(bf16[2,16,128]{2,1,0:T(8,128)(2,1)S(1)} %get-tuple-element.25.tiles, bf16[4,48,1536]{2,1,0:T(8,128)(2,1)S(1)} %get-tuple-element.38.fine_y, bf16[48,1536]{1,0:T(8,128)(2,1)S(1)} %get-tuple-element.39.cross_fine_y, ...), custom_call_target="tpu_custom_call" | custom-call | tf_op jit(solution)/shard_map/pallas_call | solution.py:364
  34.9 0.0 collective-permute-done.2.cols_b
  35.0 3.1 %collective-permute-done.3.cols_a = bf16[288,128]{1,0:T(8,128)(2,1)S(1)} collective-permute-done((bf16[288,128]{1,0:T(8,128)(2,1)S(1)}, bf16[288,128]{1,0:T(8,128)(2,1)S(1)}, u32[]{:S(2)}, u32[]{:S(2)}) %collective-permute-start.3) | collective-permute-done | bytes 73760 | tf_op jit(solution)/shard_map/ppermute | solution.py:363
  38.0 2.8 %shard_map.81 = (f32[12,4,128]{2,1,0:T(4,128)}, f32[4,256,256]{2,1,0:T(8,128)}) custom-call(s32[7]{0:T(128)S(1)} %stack.27.scalars, f32[12,4,128]{2,1,0:T(4,128)S(1)} %get-tuple-element.23.amp, f32[4,288,256]{2,1,0:T(8,128)S(1)} %get-tuple-element.30.field, f32[288,128]{1,0:T(8,128)S(1)} %get-tuple-element.31.side, ...), custom_call_target="tpu_custom_call" | custom-call | tf_op jit(solution)/shard_map/pallas_call | solution.py:371
Async XLA Ops:
  5.2 18.4 %collective-permute-start = (bf16[144,256]{1,0:T(8,128)(2,1)S(1)}, bf16[144,256]{1,0:T(8,128)(2,1)S(1)}, u32[]{:S(2)}, u32[]{:S(2)}) collective-permute-start(bf16[144,256]{1,0:T(8,128)(2,1)S(1)} %get-tuple-element.34), channel_id=1, source_target_pairs={{32,64},{64,32},{96,128},{128,96},{160,192},{192,160},{224,256},{2... | collective-permute-start | bytes 221192 | tf_op jit(solution)/shard_map/ppermute | solution.py:341
  18.8 4.8 %collective-permute-start.1 = (bf16[144,256]{1,0:T(8,128)(2,1)S(1)}, bf16[144,256]{1,0:T(8,128)(2,1)S(1)}, u32[]{:S(2)}, u32[]{:S(2)}) collective-permute-start(bf16[144,256]{1,0:T(8,128)(2,1)S(1)} %get-tuple-element.35), channel_id=1, source_target_pairs={{0,32},{32,0},{64,96},{96,64},{128,160},{160,128},{192,224},{224,1... | collective-permute-start | bytes 221192 | tf_op jit(solution)/shard_map/ppermute | solution.py:342
  24.3 10.7 %collective-permute-start.2 = (bf16[288,128]{1,0:T(8,128)(2,1)S(1)}, bf16[288,128]{1,0:T(8,128)(2,1)S(1)}, u32[]{:S(2)}, u32[]{:S(2)}) collective-permute-start(bf16[288,128]{1,0:T(8,128)(2,1)S(1)} %get-tuple-element.36), channel_id=1, source_target_pairs={{1,2},{2,1},{3,4},{4,3},{5,6},{6,5},{7,8},{8,7},{9,10},{10,9},{11,... | collective-permute-start | bytes 221192 | tf_op jit(solution)/shard_map/ppermute | solution.py:362
  31.8 6.2 %collective-permute-start.3 = (bf16[288,128]{1,0:T(8,128)(2,1)S(1)}, bf16[288,128]{1,0:T(8,128)(2,1)S(1)}, u32[]{:S(2)}, u32[]{:S(2)}) collective-permute-start(bf16[288,128]{1,0:T(8,128)(2,1)S(1)} %get-tuple-element.37.ready), channel_id=1, source_target_pairs={{0,1},{1,0},{2,3},{3,2},{4,5},{5,4},{6,7},{7,6},{8,9},{9,8},{10,11... | collective-permute-start | bytes 221192 | tf_op jit(solution)/shard_map/ppermute | solution.py:363
